TPU v7x, 32 devices: a whole 2x2x4 slice. The times are simulated.
32 devices in a mesh: blk: 8 (over z, x), sub: 4 (over y, core).
Axes of the slice: x: 2, y: 2, z: 4, core: 2. Of those that a mesh axis runs over, the one named last changes fastest.
Arguments:
- rhs: float32 [150, 98304], P(None, ('blk', 'sub')), may hold values from -6 to 6
- coeff: float32 [98304], P(('blk', 'sub')), may hold values from 0.5 to 4
- s_ref: float32 [150, 150], replicated, as said below
- m_inv: float32 [150, 150], replicated, as said below
- restriction: float32 [8, 150], replicated, may hold values from -0.5 to 0.5
- partner: int32 [8, 4], P('blk'), may hold values from 0 to 7, as said below
- counts: int32 [8, 4, 4], P('blk', 'sub'), may hold values from 96 to 192, as said below
- owner: int32 [8, 4, 16], P('blk', 'sub'), may hold values from 0 to 7, as said below
- c_inv: float32 [8, 4, 512, 512], P('blk', 'sub'), as said below
Outputs:
- solution: float32 [150, 98304], P(None, ('blk', 'sub'))
Inputs may be any that keep to these rules, and one draw needn't show every extreme that they name: For each direction pair (0, 1) and (2, 3) the column is a permutation of the blocks, and partner[partner[b, 0], 1] = b, partner[partner[b, 2], 3] = b. counts[b, s, k] = counts[partner[b, k], s, k xor 1]; the partition faces are those of the first counts[b, s, k] local elements. For every sub index, each owner block owns at most 64 aggregates, and some owner owns exactly 64. `s_ref`: symmetric positive definite. `m_inv`: symmetric positive definite. `c_inv`: each matrix symmetric positive definite.
All inputs are finite; a program needn't handle non-finite values.
Results may differ from a plain program's by a relative error of at most 0.00015.
Values sent between devices are 32-bit elements; how exact they have to be, the bound alone decides.
A program may use at most 128 MiB of HBM per device.

v0:
```python
import functools

import jax
import jax.numpy as jnp
from jax import lax
from jax.experimental import pallas as pl
from jax.experimental.pallas import tpu as pltpu
from jax.sharding import PartitionSpec as P

FACE = 25
COARSE = 8
CAP = 192
CAPO = 64
AGG = 192
LANES = 128
PER_TILE = 4
F32 = jnp.float32
BF16 = jnp.bfloat16
HIGHEST = lax.Precision.HIGHEST


def iota(shape, dim):
    return lax.broadcasted_iota(jnp.int32, shape, dim)


def halves(x):
    high = x.astype(BF16)
    return high, (x - high.astype(F32)).astype(BF16)


def thirds(x):
    high = x.astype(BF16)
    rest = x - high.astype(F32)
    mid = rest.astype(BF16)
    return high, mid, (rest - mid.astype(F32)).astype(BF16)


def product(stacked, x):
    rows = stacked.shape[0] // 2
    high, low = halves(x)
    both = jnp.dot(stacked, high, preferred_element_type=F32)
    return both[:rows] + both[rows:] + jnp.dot(stacked[:rows], low, preferred_element_type=F32)


def nt(a, b, precision=None):
    return lax.dot_general(
        a, b, (((1,), (1,)), ((), ())), precision=precision, preferred_element_type=F32
    )


def kernel(
    blocks, subs,
    partner_hbm, counts_hbm, owner_hbm,
    rhs_hbm, coeff_hbm, s_ref_hbm, m_inv_hbm, restriction_hbm, c_inv_hbm,
    held_hbm, lift_out,
    out, partner_s, counts_s, owner_s, coeff, s_ref, m_inv, restriction,
    rhs, c_inv, lhs, lhs_s, rpad, field, resid, msg1, msg3, got1, got3, y_a, y_b, got_a, got_b,
    face_msg, faces, pass_msg, passed, ends, hop, got_hop,
    s1, r1, s2, r2, s3, r3, s4, r4, sf, rf, se, re, sh, rh, sp, rp, load, load_c, load_s, keep,
):
    elements = rhs.shape[1]
    nrb = elements // AGG
    width = PER_TILE * AGG
    tiles = elements // width
    packs = blocks * nrb // LANES
    per_pack = LANES // nrb
    me = lax.axis_index("blk")
    sub = lax.axis_index("sub")
    trace = rhs.shape[0]

    loads = [
        pltpu.make_async_copy(
            rhs_hbm.at[:, pl.ds(t * width, width)], rhs.at[:, pl.ds(t * width, width)], load.at[t]
        )
        for t in range(tiles)
    ]
    small = [
        pltpu.make_async_copy(src, dst, load_s.at[i])
        for i, (src, dst) in enumerate(
            [
                (m_inv_hbm, m_inv), (restriction_hbm, restriction), (coeff_hbm, coeff),
                (s_ref_hbm, s_ref), (partner_hbm, partner_s), (counts_hbm, counts_s),
                (owner_hbm, owner_s),
            ]
        )
    ]
    for copy in small[:3] + loads + small[3:]:
        copy.start()
    load_solver = pltpu.make_async_copy(c_inv_hbm, c_inv, load_c)
    load_solver.start()
    barrier = pltpu.get_barrier_semaphore()

    def greet(i, carry):
        pl.semaphore_signal(
            barrier, inc=1, device_id={"blk": lax.rem(me + i, blocks)},
            device_id_type=pl.DeviceIdType.MESH,
        )
        return carry

    lax.fori_loop(1, blocks, greet, 0)

    @pl.when(sub > 0)
    def _():
        pl.semaphore_signal(
            barrier, inc=1, device_id={"sub": sub - 1}, device_id_type=pl.DeviceIdType.MESH
        )

    @pl.when(sub < subs - 1)
    def _():
        pl.semaphore_signal(
            barrier, inc=1, device_id={"sub": sub + 1}, device_id_type=pl.DeviceIdType.MESH
        )

    def spread(src, dst, send, recv):
        def one(i, carry):
            peer = lax.rem(me + i, blocks)
            pltpu.make_async_remote_copy(
                src_ref=src, dst_ref=dst.at[me], send_sem=send.at[peer], recv_sem=recv.at[me],
                device_id={"blk": peer}, device_id_type=pl.DeviceIdType.MESH,
            ).start()
            return carry

        lax.fori_loop(1, blocks, one, 0)

    def handle(src, dst, send, recv, peer):
        return pltpu.make_async_remote_copy(
            src_ref=src, dst_ref=dst.at[peer], send_sem=send.at[peer], recv_sem=recv.at[peer],
            device_id={"blk": peer}, device_id_type=pl.DeviceIdType.MESH,
        )

    def collect(src, dst, send, recv):
        def one(i, carry):
            handle(src, dst, send, recv, lax.rem(me + i, blocks)).wait_recv()
            return carry

        lax.fori_loop(1, blocks, one, 0)

    def sent(src, dst, send, recv):
        def one(i, carry):
            handle(src, dst, send, recv, lax.rem(me + i, blocks)).wait_send()
            return carry

        lax.fori_loop(1, blocks, one, 0)

    def beside(src, dst, slot, send, recv, peer):
        return pltpu.make_async_remote_copy(
            src_ref=src, dst_ref=dst.at[slot], send_sem=send.at[slot], recv_sem=recv.at[slot],
            device_id={"sub": peer}, device_id_type=pl.DeviceIdType.MESH,
        )

    for copy in small[:3]:
        copy.wait()
    lhs[0:trace] = m_inv[...]
    lhs[trace:152] = jnp.zeros((152 - trace, trace), F32)
    lhs[152:160] = restriction[...]
    both = lhs[...]
    high, low = halves(both)
    stack_m = jnp.concatenate([high, low], 0)
    rpad[...] = jnp.zeros((COARSE, 256), F32)
    rpad[:, 0:trace] = restriction[...]
    spread_r = rpad[...]
    backward = pltpu.roll(spread_r, 256 - FACE, 1)
    forward = pltpu.roll(spread_r, FACE, 1)
    r_lane = iota((COARSE, 256), 1)

    def at(slot, from_slot):
        moved = backward if from_slot > slot else forward
        inside = (r_lane >= slot * FACE) & (r_lane < (slot + 1) * FACE)
        return jnp.where(inside, moved, 0.0)

    low_part, high_part = at(4, 5), at(5, 4)
    sides = [at(k, k ^ 1) for k in range(4)]
    high, low = halves(jnp.concatenate(sides, 0)[:, :trace])
    stack_l = jnp.concatenate([high, low], 0)

    lane = iota((COARSE, LANES), 1)
    wide_lane = iota((COARSE, width), 1)

    def gather_lanes(values, total, tile):
        for a in range(PER_TILE):
            inside = (wide_lane >= a * AGG) & (wide_lane < (a + 1) * AGG)
            part = jnp.sum(jnp.where(inside, values, 0.0), 1, keepdims=True)
            total = jnp.where(lane == tile * PER_TILE + a, part, total)
        return total

    def spread_lanes(values, tile, rows):
        where = iota((rows, width), 1)
        first = tile * PER_TILE
        wide = jnp.broadcast_to(values[:, first + PER_TILE - 1 : first + PER_TILE], (rows, width))
        for a in range(PER_TILE - 2, -1, -1):
            wide = jnp.where(
                where < (a + 1) * AGG, values[:, first + a : first + a + 1], wide
            )
        return wide

    zero_tile = jnp.zeros((COARSE, LANES), F32)
    sums = zero_tile
    coeff_sums = zero_tile
    for tile in range(tiles):
        cols = slice(tile * width, (tile + 1) * width)
        loads[tile].wait()
        made = product(stack_m, rhs[:, cols])
        c_row = coeff[:, cols]
        field[:, LANES + tile * width : LANES + (tile + 1) * width] = made[:152] * (0.5 / c_row)
        sums = gather_lanes(made[152:160], sums, tile)
        coeff_sums = gather_lanes(
            jnp.broadcast_to(c_row, (COARSE, width)), coeff_sums, tile
        )

    def place(values):
        values = jnp.where(lane < nrb, values, 0.0)
        return pltpu.roll(values, lax.rem(me, per_pack) * nrb, 1)

    for copy in small[3:]:
        copy.wait()
    lhs_s[0:trace] = s_ref[...]
    lhs_s[trace:160] = jnp.zeros((160 - trace, trace), F32)
    high, low = halves(lhs_s[...])
    stack_s = jnp.concatenate([high, low], 0)
    side_lane = iota((COARSE, 256), 1)
    side_sums = zero_tile
    made = product(stack_l, field[0:trace, LANES : LANES + 256])
    for k in range(4):
        part = jnp.where(side_lane < counts_s[0, k], made[8 * k : 8 * k + 8], 0.0)
        side_sums = jnp.where(lane == k, jnp.sum(part, 1, keepdims=True), side_sums)
    owner_tile = zero_tile
    row8 = iota((COARSE, LANES), 0)
    for g in range(nrb):
        owner_tile = jnp.where(lane == g, owner_s[0, g].astype(F32), owner_tile)
    for k in range(4):
        owner_tile = jnp.where(
            (row8 == 1) & (lane == k), partner_s[0, k].astype(F32), owner_tile
        )
        owner_tile = jnp.where(
            (row8 == 2) & (lane == k), counts_s[0, k].astype(F32), owner_tile
        )
    owner_tile = jnp.where(row8 == 3, coeff_sums, owner_tile)
    msg1[0:8] = place(sums)
    msg1[8:16] = place(owner_tile)
    msg1[16:24] = place(side_sums)
    got1[me] = msg1[...]

    pl.semaphore_wait(
        barrier,
        blocks - 1 + (sub > 0).astype(jnp.int32) + (sub < subs - 1).astype(jnp.int32),
    )
    spread(msg1, got1, s1, r1)

    lines = blocks // 2
    line = me // 2
    side = lax.rem(me, 2)
    mate = me + 1 - 2 * side
    head = field[0:104, LANES : 2 * LANES]
    tail = field[0:104, 2 * LANES : 3 * LANES]
    half = iota((56, LANES), 1) < LANES // 2
    turned = pltpu.roll(tail, LANES // 2, 1)
    upper = jnp.concatenate([turned[56:104], jnp.zeros((8, LANES), F32)], 0)
    face_msg[0:104] = head
    face_msg[104:160] = jnp.where(half, tail[0:56], upper)
    faces[line] = face_msg[...]

    def face_copy(place_at, peer):
        return pltpu.make_async_remote_copy(
            src_ref=face_msg, dst_ref=faces.at[place_at], send_sem=sf.at[peer],
            recv_sem=rf.at[place_at], device_id={"blk": peer * 2 + side},
            device_id_type=pl.DeviceIdType.MESH,
        )

    def send_faces(offset):
        face_copy(line, lax.rem(line + offset, lines)).start()

    pass_copy = pltpu.make_async_remote_copy(
        src_ref=pass_msg, dst_ref=passed, send_sem=sp, recv_sem=rp,
        device_id={"blk": mate}, device_id_type=pl.DeviceIdType.MESH,
    )
    first_src = field.at[96:152, LANES : 2 * LANES]
    last_src = field.at[96:152, elements : elements + LANES]

    @pl.when(sub < subs - 1)
    def _():
        beside(last_src, ends, 0, se, re, sub + 1).start()

    @pl.when(sub > 0)
    def _():
        beside(first_src, ends, 1, se, re, sub - 1).start()

    early = [1, lines - 1] if lines > 2 else [1]
    for offset in early:
        send_faces(offset)

    row56 = iota((56, width), 0)

    def second(tile, total):
        cols = slice(tile * width, (tile + 1) * width)
        u = field[:, LANES + tile * width : LANES + (tile + 1) * width]
        su = product(stack_s, u[:trace])
        c_row = coeff[:, cols]
        resid[0:trace] = rhs[:, cols] - su[:trace] * c_row - u[:trace]
        wide = field[96:152, tile * width : (tile + 1) * width + 2 * LANES]
        span = width + 2 * LANES
        below = pltpu.roll(wide, 1, 1)[:, LANES : LANES + width]
        above = pltpu.roll(wide, span - 1, 1)[:, LANES : LANES + width]
        below = pltpu.roll(below, 56 - FACE, 0)
        above = pltpu.roll(above, FACE, 0)
        column = jnp.where(
            (row56 >= 4) & (row56 < 4 + FACE), below,
            jnp.where((row56 >= 4 + FACE) & (row56 < 4 + 2 * FACE), above, 0.0),
        )
        resid[96:152] = resid[96:152] + column
        made = product(stack_m, resid[0:trace])
        out[:, cols] = u[:trace] + made[:trace] * (0.5 / c_row)
        return gather_lanes(made[152:160], total, tile)

    sums_two = zero_tile
    for tile in range(1, tiles - 1):
        sums_two = second(tile, sums_two)

    @pl.when(sub > 0)
    def _():
        beside(last_src, ends, 0, se, re, sub - 1).wait_recv()
        field[96:152, 0:LANES] = ends[0]

    @pl.when(sub == 0)
    def _():
        field[96:152, 0:LANES] = jnp.zeros((56, LANES), F32)

    @pl.when(sub < subs - 1)
    def _():
        beside(first_src, ends, 1, se, re, sub + 1).wait_recv()
        field[96:152, LANES + elements : 2 * LANES + elements] = ends[1]

    @pl.when(sub == subs - 1)
    def _():
        field[96:152, LANES + elements : 2 * LANES + elements] = jnp.zeros((56, LANES), F32)

    sums_two = second(tiles - 1, sums_two)

    collect(msg1, got1, s1, r1)

    def packed(got):
        return [
            jnp.sum(got[t * per_pack : (t + 1) * per_pack], 0) for t in range(packs)
        ]

    first_pack = packed(got1)
    owner_rows = [p[8:9] for p in first_pack]
    eye = iota((LANES, LANES), 0) == iota((LANES, LANES), 1)
    earlier = iota((LANES, LANES), 0) < iota((LANES, LANES), 1)
    owner_cols = [
        jnp.sum(jnp.where(eye, row, 0.0), 1, keepdims=True) for row in owner_rows
    ]
    slot_rows = []
    for t in range(packs):
        slot = jnp.zeros((1, LANES), F32)
        for before in range(t + 1):
            same = owner_cols[before] == owner_rows[t]
            if before == t:
                same = same & earlier
            slot = slot + jnp.sum(jnp.where(same, 1.0, 0.0), 0, keepdims=True)
        slot_rows.append(slot)
    order = COARSE * CAPO
    slot_of = (iota((order, LANES), 0) // COARSE).astype(F32)
    me_real = me.astype(F32)
    slotted = [jnp.where(slot_of == slot_rows[t], 1.0, 0.0).astype(BF16) for t in range(packs)]
    chosen = [
        jnp.where((slot_of == slot_rows[t]) & (owner_rows[t] == me_real), 1.0, 0.0).astype(BF16)
        for t in range(packs)
    ]
    pick = lax.rem(iota((order, 3 * COARSE), 0), COARSE) == lax.rem(
        iota((order, 3 * COARSE), 1), COARSE
    )

    def solve(packs_of):
        wide = jnp.zeros((order, 3 * COARSE), F32)
        for t in range(packs):
            wide = wide + nt(chosen[t], jnp.concatenate(thirds(packs_of[t]), 0))
        column = jnp.sum(jnp.where(pick, wide, 0.0), 1, keepdims=True)
        return jnp.sum(c_inv[...] * column, 0, keepdims=True)

    load_solver.wait()
    y_a[...] = solve([p[0:8] for p in first_pack])
    got_a[me] = y_a[...]
    spread(y_a, got_a, s2, r2)

    target = jnp.where(lane < nrb, me * nrb + lane, -1)
    for k in range(4):
        target = jnp.where(lane == nrb + k, partner_s[0, k] * nrb, target)
    found = jnp.zeros((COARSE, LANES), F32)
    own_sel = []
    toward = jnp.full((COARSE, LANES), -1, jnp.int32)
    for k in range(4):
        toward = jnp.where(lane == k, partner_s[0, k] * nrb + (k ^ 1), toward)
    side_found = jnp.zeros((3 * COARSE, LANES), F32)
    for t in range(packs):
        sel = iota((LANES, LANES), 0) + t * LANES == toward[0:1]
        side_found = side_found + jnp.dot(
            jnp.concatenate(thirds(first_pack[t][16:24]), 0),
            jnp.where(sel, 1.0, 0.0).astype(BF16), preferred_element_type=F32,
        )
    side_found = side_found[0:8] + side_found[8:16] + side_found[16:24]
    sides_in = jnp.sum(jnp.where(lane < 4, side_found, 0.0), 1, keepdims=True)
    sums_two = second(0, sums_two)
    sums_two = sums_two + jnp.where(lane == 0, sides_in, 0.0)
    msg3[...] = place(sums_two)
    got3[me] = msg3[...]
    spread(msg3, got3, s3, r3)
    for offset in range(2, lines - 1):
        send_faces(offset)

    base = jnp.concatenate(
        [nt(restriction[...], s_ref[...], HIGHEST)]
        + [
            part[:, :trace]
            for part in [spread_r - low_part - high_part, low_part, high_part] + sides
        ],
        0,
    )
    unit = jnp.where(iota((152, trace), 0) == iota((152, trace), 1), 1.0, 0.0)
    lifted = nt(
        unit,
        jnp.concatenate([restriction[...], jnp.zeros((7 * COARSE, trace), F32)], 0),
        HIGHEST,
    )
    weights = nt(both, base, HIGHEST)
    signs = jnp.where(iota((152, 8 * COARSE), 1) < 4 * COARSE, -0.5, 0.5)
    correct = lifted + weights[:152] * signs
    high, low = halves(correct)
    stack_x = jnp.concatenate([high, low], 0)
    reduced = weights[152:160]

    for t in range(packs):
        sel = iota((LANES, LANES), 0) + t * LANES == target[0:1]
        own_sel.append(jnp.where(sel, 1.0, 0.0).astype(BF16))
        pair = jnp.where(row8 == 0, owner_rows[t], slot_rows[t])
        found = found + jnp.dot(
            pair.astype(BF16), own_sel[t], preferred_element_type=F32
        )
    owner_sel, slot_sel = found[0:1], found[1:2]
    back = jnp.where(slot_of == slot_sel, 1.0, 0.0).astype(BF16)
    block_of = iota((blocks, COARSE, LANES), 0).astype(F32)
    keep_row = (
        iota((blocks, COARSE, order), 1) == lax.rem(iota((blocks, COARSE, order), 2), COARSE)
    )

    def rows_of(got):
        rows = jnp.where(keep_row, got[...], 0.0).reshape(blocks * COARSE, order)
        return jnp.concatenate(thirds(rows), 0)

    def fetch(rows, at_slot, owner_row):
        made = jnp.dot(rows, at_slot, preferred_element_type=F32)
        count = blocks * COARSE
        made = made[:count] + made[count : 2 * count] + made[2 * count :]
        made = made.reshape(blocks, COARSE, LANES)
        return jnp.sum(jnp.where(block_of == owner_row[None], made, 0.0), 0)

    def picked(values, onehots):
        count = values[0].shape[0]
        total = jnp.zeros((3 * count, LANES), F32)
        for value, onehot in zip(values, onehots):
            total = total + jnp.dot(
                jnp.concatenate(thirds(value), 0), onehot, preferred_element_type=F32
            )
        return total[:count] + total[count : 2 * count] + total[2 * count :]

    in_block = lax.rem(lane, nrb)
    side_sel = [
        [
            jnp.where(
                (iota((LANES, LANES), 0) + source * LANES).astype(F32)
                == first_pack[t][9:10] * float(nrb),
                1.0, 0.0,
            ).astype(BF16)
            for source in range(packs)
        ]
        for t in range(packs)
    ]

    collect(y_a, got_a, s2, r2)
    rows = rows_of(got_a)
    omegas = [0.5 * fetch(rows, slotted[t], owner_rows[t]) for t in range(packs)]
    for t in range(packs):
        hop[t] = omegas[t]

    @pl.when(sub < subs - 1)
    def _():
        beside(hop, got_hop, 0, sh, rh, sub + 1).start()

    @pl.when(sub > 0)
    def _():
        beside(hop, got_hop, 1, sh, rh, sub - 1).start()

    crossed = [picked(omegas, side_sel[t]) for t in range(packs)]

    @pl.when(sub > 0)
    def _():
        beside(hop, got_hop, 0, sh, rh, sub - 1).wait_recv()

    @pl.when(sub == 0)
    def _():
        got_hop[0] = jnp.zeros((packs, COARSE, LANES), F32)

    @pl.when(sub < subs - 1)
    def _():
        beside(hop, got_hop, 1, sh, rh, sub + 1).wait_recv()

    @pl.when(sub == subs - 1)
    def _():
        got_hop[1] = jnp.zeros((packs, COARSE, LANES), F32)

    collect(msg3, got3, s3, r3)
    base_sums = packed(got3)
    states = []
    seconds = []
    for t in range(packs):
        omega = omegas[t]
        before = jnp.where(
            in_block == 0,
            pltpu.roll(got_hop[0, t], LANES - (nrb - 1), 1), pltpu.roll(omega, 1, 1),
        )
        after = jnp.where(
            in_block == nrb - 1,
            pltpu.roll(got_hop[1, t], nrb - 1, 1), pltpu.roll(omega, LANES - 1, 1),
        )
        step_down = omega - before
        step_up = omega - after
        values = [omega * first_pack[t][11:12], float(AGG) * omega, step_down, step_up]
        share = crossed[t] * (-first_pack[t][10:11])
        for k in range(4):
            moved = share if k == 0 else pltpu.roll(share, LANES - k, 1)
            values.append(jnp.where(in_block == 0, moved, 0.0))
        change = jnp.dot(
            reduced, jnp.concatenate(values, 0), precision=HIGHEST, preferred_element_type=F32
        )
        seconds.append(base_sums[t] - change)
        states.append(jnp.concatenate([omega, step_down, step_up], 0))
    y_b[...] = solve(seconds)
    got_b[me] = y_b[...]
    spread(y_b, got_b, s4, r4)

    state = picked(states, own_sel)
    omega, step_down, step_up = state[0:8], state[8:16], state[16:24]
    across = [omega[:, nrb + k : nrb + k + 1] for k in range(4)]

    packed_row = iota((160, LANES), 0)
    face_row = jnp.where(
        packed_row < 104, packed_row,
        jnp.where(iota((160, LANES), 1) < LANES // 2, packed_row - 104, packed_row - 48),
    )

    def sources(of):
        wanted = jnp.full((160, LANES), -1.0, F32)
        for q in range(4):
            inside = (face_row >= q * FACE) & (face_row < (q + 1) * FACE)
            wanted = jnp.where(inside, of[q ^ 1], wanted)
        return wanted

    side_real = side.astype(F32)

    def from_line(wanted, start):
        for z in range(lines):
            start = jnp.where(wanted == 2.0 * z + side_real, faces[z], start)
        return start

    for offset in range(1, lines):
        face_copy(lax.rem(line + offset, lines), lax.rem(line + offset, lines)).wait_recv()
    mates = []
    for k in range(4):
        total = jnp.zeros((1, 1), F32)
        for t in range(packs):
            here = lane[0:1] + t * LANES == mate * nrb + k
            total = total + jnp.sum(
                jnp.where(here, first_pack[t][9:10], 0.0), 1, keepdims=True
            )
        mates.append(total)
    pass_msg[...] = from_line(sources(mates), jnp.zeros((160, LANES), F32))
    pass_copy.start()

    def lateral_change():
        pass_copy.wait_recv()
        wanted = sources([partner_s[0, k].astype(F32) for k in range(4)])
        taken = from_line(wanted, passed[...])
        unfolded = taken[104:160]
        turned = pltpu.roll(unfolded, LANES // 2, 1)
        wide = jnp.concatenate(
            [taken[0:104], jnp.concatenate([unfolded, turned[0:48]], 0)], 1
        )
        backward = pltpu.roll(wide, 104 - FACE, 0)
        forward = pltpu.roll(wide, FACE, 0)
        row = iota((104, 256), 0)
        col = iota((104, 256), 1)
        lateral = jnp.zeros((104, 256), F32)
        for k in range(4):
            inside = (row >= k * FACE) & (row < (k + 1) * FACE) & (col < counts_s[0, k])
            lateral = jnp.where(inside, backward if k % 2 == 0 else forward, lateral)
        made = product(stack_m[:, :104], lateral)
        out[:, 0:256] = out[:, 0:256] + made[:trace] * (0.5 / coeff[:, 0:256])

    def coarse_change(tile):
        cols = slice(tile * width, (tile + 1) * width)
        inverse = 1.0 / coeff[:, cols]
        step = lax.rem(wide_lane, AGG)
        here = spread_lanes(omega, tile, COARSE)
        scaled = here * inverse
        down = jnp.where(step == 0, spread_lanes(step_down, tile, COARSE) * inverse, 0.0)
        up = jnp.where(step == AGG - 1, spread_lanes(step_up, tile, COARSE) * inverse, 0.0)
        rows = [here, scaled, down, up]
        if tile == 0:
            for k in range(4):
                rows.append(jnp.where(wide_lane < counts_s[0, k], across[k] * inverse, 0.0))
            made = product(stack_x, jnp.concatenate(rows, 0))
        else:
            made = product(stack_x[:, : 4 * COARSE], jnp.concatenate(rows, 0))
        out[:, cols] = out[:, cols] + made[:trace]

    keeps = [
        pltpu.make_async_copy(
            out.at[:, pl.ds(t * width, width)], held_hbm.at[:, pl.ds(t * width, width)], keep.at[t]
        )
        for t in range(tiles)
    ]
    for tile in range(1, tiles):
        coarse_change(tile)
        keeps[tile].start()
    coarse_change(0)
    lateral_change()
    keeps[0].start()

    sent(msg1, got1, s1, r1)
    for offset in range(1, lines):
        face_copy(line, lax.rem(line + offset, lines)).wait_send()
    pass_copy.wait_send()
    sent(y_a, got_a, s2, r2)
    sent(msg3, got3, s3, r3)

    @pl.when(sub < subs - 1)
    def _():
        beside(last_src, ends, 0, se, re, sub + 1).wait_send()
        beside(hop, got_hop, 0, sh, rh, sub + 1).wait_send()

    @pl.when(sub > 0)
    def _():
        beside(first_src, ends, 1, se, re, sub - 1).wait_send()
        beside(hop, got_hop, 1, sh, rh, sub - 1).wait_send()

    collect(y_b, got_b, s4, r4)
    final = 0.5 * fetch(rows_of(got_b), back, owner_sel)
    lift_out[...] = jnp.dot(
        lifted[:, 0:COARSE], final, precision=HIGHEST, preferred_element_type=F32
    )
    sent(y_b, got_b, s4, r4)
    for copy in keeps:
        copy.wait()


def finish(lift_hbm, held_hbm, out_hbm, lift, held, done, load_lift, load, store):
    rows, elements = held.shape
    width = 2 * AGG
    tiles = elements // width
    loads, stores = [], []
    for t in range(tiles):
        cols = pl.ds(t * width, width)
        loads.append(pltpu.make_async_copy(held_hbm.at[:, cols], held.at[:, cols], load.at[t]))
        stores.append(pltpu.make_async_copy(done.at[:, cols], out_hbm.at[:, cols], store.at[t]))
    first_load = pltpu.make_async_copy(lift_hbm, lift, load_lift)
    first_load.start()
    for copy in loads:
        copy.start()
    first_load.wait()
    split = iota((rows, LANES), 1) < LANES // 2
    for t in range(tiles):
        first = jnp.broadcast_to(lift[:rows, 2 * t : 2 * t + 1], (rows, LANES))
        second = jnp.broadcast_to(lift[:rows, 2 * t + 1 : 2 * t + 2], (rows, LANES))
        left, mid, right = (pl.ds(t * width + q * LANES, LANES) for q in range(3))
        loads[t].wait()
        done[:, left] = held[:, left] + first
        done[:, mid] = held[:, mid] + jnp.where(split, first, second)
        done[:, right] = held[:, right] + second
        stores[t].start()
    for copy in stores:
        copy.wait()


def per_device(blocks, subs, rhs, coeff, s_ref, m_inv, restriction, partner, counts, owner, c_inv):
    trace, elements = rhs.shape
    width = PER_TILE * AGG
    order = COARSE * CAPO
    vmem = pl.BlockSpec(memory_space=pltpu.VMEM)
    packs = blocks * owner.shape[2] // LANES
    far = pl.BlockSpec(memory_space=pltpu.HBM)
    dma = pltpu.SemaphoreType.DMA
    held, lift = pl.pallas_call(
        functools.partial(kernel, blocks, subs),
        out_shape=(
            jax.ShapeDtypeStruct((trace, elements), F32),
            jax.ShapeDtypeStruct((152, LANES), F32),
        ),
        in_specs=[far] * 9,
        out_specs=(far, vmem),
        scratch_shapes=[
            pltpu.VMEM((trace, elements), F32),
            pltpu.SMEM((1, 4), jnp.int32),
            pltpu.SMEM((1, 4), jnp.int32),
            pltpu.SMEM((1, owner.shape[2]), jnp.int32),
            pltpu.VMEM((1, elements), F32),
            pltpu.VMEM((trace, trace), F32),
            pltpu.VMEM((trace, trace), F32),
            pltpu.VMEM((COARSE, trace), F32),
            pltpu.VMEM((trace, elements), F32),
            pltpu.VMEM((order, order), F32),
            pltpu.VMEM((160, trace), F32),
            pltpu.VMEM((160, trace), F32),
            pltpu.VMEM((8, 256), F32),
            pltpu.VMEM((152, elements + 2 * LANES), F32),
            pltpu.VMEM((152, width), F32),
            pltpu.VMEM((24, LANES), F32),
            pltpu.VMEM((8, LANES), F32),
            pltpu.VMEM((blocks, 24, LANES), F32),
            pltpu.VMEM((blocks, 8, LANES), F32),
            pltpu.VMEM((1, order), F32),
            pltpu.VMEM((1, order), F32),
            pltpu.VMEM((blocks, 1, order), F32),
            pltpu.VMEM((blocks, 1, order), F32),
            pltpu.VMEM((160, LANES), F32),
            pltpu.VMEM((blocks // 2, 160, LANES), F32),
            pltpu.VMEM((160, LANES), F32),
            pltpu.VMEM((160, LANES), F32),
            pltpu.VMEM((2, 56, LANES), F32),
            pltpu.VMEM((packs, 8, LANES), F32),
            pltpu.VMEM((2, packs, 8, LANES), F32),
        ]
        + [dma((blocks,))] * 8
        + [dma((blocks // 2,))] * 2
        + [dma((2,))] * 4
        + [dma, dma, dma((elements // width,)), dma, dma((7,)), dma((elements // width,))],
        compiler_params=pltpu.CompilerParams(
            collective_id=0, has_side_effects=True
        ),
    )(
        partner, counts[0], owner[0], rhs, coeff[None, :], s_ref, m_inv, restriction, c_inv[0, 0],
    )
    pairs = elements // (2 * AGG)
    return pl.pallas_call(
        finish,
        out_shape=jax.ShapeDtypeStruct((trace, elements), F32),
        in_specs=[far, far],
        out_specs=far,
        scratch_shapes=[
            pltpu.VMEM((152, LANES), F32),
            pltpu.VMEM((trace, elements), F32),
            pltpu.VMEM((trace, elements), F32),
            dma,
            dma((pairs,)),
            dma((pairs,)),
        ],
    )(lift, held)


def solution(mesh):
    in_specs = (
        P(None, ("blk", "sub")),
        P(("blk", "sub")),
        P(),
        P(),
        P(),
        P("blk", None),
        P("blk", "sub", None),
        P("blk", "sub", None),
        P("blk", "sub", None, None),
    )
    out_specs = P(None, ("blk", "sub"))
    body = functools.partial(per_device, mesh.shape["blk"], mesh.shape["sub"])
    return jax.shard_map(
        body, mesh=mesh, in_specs=in_specs, out_specs=out_specs, check_vma=False
    )
```

profile of v0, /device:TPU:0, one launch (start us, length us, event | category | flops | bytes accessed | tf_op | source)
XLA Modules:
  0.0 29.2 jit_solution(4840218433764759989)
XLA Ops:
  0.0 25.9 %shard_map.91 = (f32[150,3072]{1,0:T(8,128)}, f32[152,128]{1,0:T(8,128)}) custom-call(s32[1,4]{1,0:T(1,128)} %partner_hbm.1, s32[1,4]{1,0:T(1,128)} %bitcast.6, s32[1,16]{1,0:T(1,128)} %bitcast.7, f32[150,3072]{1,0:T(8,128)} %rhs_hbm.1, f32[1,3072]{1,0:T(1,128)} %bitcast.5, f32[150,150]{1,0:T(8,128)} %s_ref_hbm.1, f32[150,150]{1,0:T(8,128)} %m_inv_hbm.1, ...), custom_call_target="tpu_custom_call" | custom-call | tf_op jit(solution)/shard_map/pallas_call | solution.py:691
  25.9 3.3 %shard_map.92 = f32[150,3072]{1,0:T(8,128)} custom-call(f32[152,128]{1,0:T(8,128)} %get-tuple-element.7.lift_hbm, f32[150,3072]{1,0:T(8,128)} %get-tuple-element.8.held_hbm), custom_call_target="tpu_custom_call" | custom-call | tf_op jit(solution)/shard_map/pallas_call | solution.py:742
where the time goes:
time: 29.3 us; the launch traced here: 29.2 us
  Pallas kernels  29.2 us (100%)
    pallas_call x1, Pallas kernels, per_device(): pl.pallas_call(functools.partial(kernel, blocks, subs), out_shape=(jax.Sh...  25.9 us
    pallas_call x1, Pallas kernels, per_device(): pl.pallas_call(finish, out_shape=jax.ShapeDtypeStruct((trace, elements),...  3.27 us

commit v1 on v0

--- a/solution.py
+++ b/solution.py
@@ -52,11 +52,11 @@
     blocks, subs,
     partner_hbm, counts_hbm, owner_hbm,
     rhs_hbm, coeff_hbm, s_ref_hbm, m_inv_hbm, restriction_hbm, c_inv_hbm,
-    held_hbm, lift_out,
-    out, partner_s, counts_s, owner_s, coeff, s_ref, m_inv, restriction,
+    out, lift_out,
+    partner_s, counts_s, owner_s, coeff, s_ref, m_inv, restriction,
     rhs, c_inv, lhs, lhs_s, rpad, field, resid, msg1, msg3, got1, got3, y_a, y_b, got_a, got_b,
     face_msg, faces, pass_msg, passed, ends, hop, got_hop,
-    s1, r1, s2, r2, s3, r3, s4, r4, sf, rf, se, re, sh, rh, sp, rp, load, load_c, load_s, keep,
+    s1, r1, s2, r2, s3, r3, s4, r4, sf, rf, se, re, sh, rh, sp, rp, load, load_c, load_s,
 ):
     elements = rhs.shape[1]
     nrb = elements // AGG
@@ -612,18 +612,10 @@
             made = product(stack_x[:, : 4 * COARSE], jnp.concatenate(rows, 0))
         out[:, cols] = out[:, cols] + made[:trace]
 
-    keeps = [
-        pltpu.make_async_copy(
-            out.at[:, pl.ds(t * width, width)], held_hbm.at[:, pl.ds(t * width, width)], keep.at[t]
-        )
-        for t in range(tiles)
-    ]
     for tile in range(1, tiles):
         coarse_change(tile)
-        keeps[tile].start()
     coarse_change(0)
     lateral_change()
-    keeps[0].start()
 
     sent(msg1, got1, s1, r1)
     for offset in range(1, lines):
@@ -648,30 +640,21 @@
         lifted[:, 0:COARSE], final, precision=HIGHEST, preferred_element_type=F32
     )
     sent(y_b, got_b, s4, r4)
-    for copy in keeps:
-        copy.wait()
-
-
-def finish(lift_hbm, held_hbm, out_hbm, lift, held, done, load_lift, load, store):
+
+
+def finish(lift, held, out_hbm, done, store):
     rows, elements = held.shape
     width = 2 * AGG
     tiles = elements // width
-    loads, stores = [], []
+    stores = []
     for t in range(tiles):
         cols = pl.ds(t * width, width)
-        loads.append(pltpu.make_async_copy(held_hbm.at[:, cols], held.at[:, cols], load.at[t]))
         stores.append(pltpu.make_async_copy(done.at[:, cols], out_hbm.at[:, cols], store.at[t]))
-    first_load = pltpu.make_async_copy(lift_hbm, lift, load_lift)
-    first_load.start()
-    for copy in loads:
-        copy.start()
-    first_load.wait()
     split = iota((rows, LANES), 1) < LANES // 2
     for t in range(tiles):
         first = jnp.broadcast_to(lift[:rows, 2 * t : 2 * t + 1], (rows, LANES))
         second = jnp.broadcast_to(lift[:rows, 2 * t + 1 : 2 * t + 2], (rows, LANES))
         left, mid, right = (pl.ds(t * width + q * LANES, LANES) for q in range(3))
-        loads[t].wait()
         done[:, left] = held[:, left] + first
         done[:, mid] = held[:, mid] + jnp.where(split, first, second)
         done[:, right] = held[:, right] + second
@@ -691,13 +674,12 @@
     held, lift = pl.pallas_call(
         functools.partial(kernel, blocks, subs),
         out_shape=(
-            jax.ShapeDtypeStruct((trace, elements), F32),
-            jax.ShapeDtypeStruct((152, LANES), F32),
+            pltpu.VMEM((trace, elements), F32),
+            pltpu.VMEM((152, LANES), F32),
         ),
         in_specs=[far] * 9,
-        out_specs=(far, vmem),
+        out_specs=(vmem, vmem),
         scratch_shapes=[
-            pltpu.VMEM((trace, elements), F32),
             pltpu.SMEM((1, 4), jnp.int32),
             pltpu.SMEM((1, 4), jnp.int32),
             pltpu.SMEM((1, owner.shape[2]), jnp.int32),
@@ -731,7 +713,7 @@
         + [dma((blocks,))] * 8
         + [dma((blocks // 2,))] * 2
         + [dma((2,))] * 4
-        + [dma, dma, dma((elements // width,)), dma, dma((7,)), dma((elements // width,))],
+        + [dma, dma, dma((elements // width,)), dma, dma((7,))],
         compiler_params=pltpu.CompilerParams(
             collective_id=0, has_side_effects=True
         ),
@@ -742,17 +724,13 @@
     return pl.pallas_call(
         finish,
         out_shape=jax.ShapeDtypeStruct((trace, elements), F32),
-        in_specs=[far, far],
+        in_specs=[vmem, vmem],
         out_specs=far,
         scratch_shapes=[
-            pltpu.VMEM((152, LANES), F32),
             pltpu.VMEM((trace, elements), F32),
-            pltpu.VMEM((trace, elements), F32),
-            dma,
-            dma((pairs,)),
             dma((pairs,)),
         ],
-    )(lift, held)
+    )(*[pltpu.with_memory_space_constraint(v, pltpu.VMEM) for v in (lift, held)])
 
 
 def solution(mesh):

time: 29.3 us -> 26.8 us (0.915)
  Pallas kernels: 29.2 us -> 26.7 us
    pallas_call x1, Pallas kernels: 3.27 us -> 1.4 us  [per_device(): pl.pallas_call(finish, out_shape=jax.ShapeDtypeStruct((trace, elements),...]
    pallas_call x1, Pallas kernels: 25.9 us -> 25.3 us  [per_device(): pl.pallas_call(functools.partial(kernel, blocks, subs), out_shape=(pltpu....]
where the time goes in v1:
time: 26.8 us; the launch traced here: 26.7 us
  Pallas kernels  26.7 us (100%)
    pallas_call x1, Pallas kernels, per_device(): pl.pallas_call(functools.partial(kernel, blocks, subs), out_shape=(pltpu....  25.3 us
    pallas_call x1, Pallas kernels, per_device(): pl.pallas_call(finish, out_shape=jax.ShapeDtypeStruct((trace, elements),...  1.4 us

profile of v1, /device:TPU:0, one launch (start us, length us, event | category | flops | bytes accessed | tf_op | source)
XLA Modules:
  0.0 26.7 jit_solution(15997749419377088780)
XLA Ops:
  0.0 25.3 %shard_map.91 = (f32[150,3072]{1,0:T(8,128)S(1)}, f32[152,128]{1,0:T(8,128)S(1)}) custom-call(s32[1,4]{1,0:T(1,128)} %partner_hbm.1, s32[1,4]{1,0:T(1,128)} %bitcast.6, s32[1,16]{1,0:T(1,128)} %bitcast.7, f32[150,3072]{1,0:T(8,128)} %rhs_hbm.1, f32[1,3072]{1,0:T(1,128)} %bitcast.5, f32[150,150]{1,0:T(8,128)} %s_ref_hbm.1, f32[150,150]{1,0:T(8,128)} %m_inv_hbm.1, ...), custom_call_target="tpu_custom_call" | custom-call | tf_op jit(solution)/shard_map/pallas_call | solution.py:674
  25.3 1.4 %shard_map.92 = f32[150,3072]{1,0:T(8,128)} custom-call(f32[152,128]{1,0:T(8,128)S(1)} %get-tuple-element.7.lift, f32[150,3072]{1,0:T(8,128)S(1)} %get-tuple-element.8.held), custom_call_target="tpu_custom_call" | custom-call | tf_op jit(solution)/shard_map/pallas_call | solution.py:724

commit v2 on v1

v2 whole, which is shorter than its diff:
```python
import functools

import jax
import jax.numpy as jnp
from jax import lax
from jax.experimental import pallas as pl
from jax.experimental.pallas import tpu as pltpu
from jax.sharding import PartitionSpec as P

FACE = 25
COARSE = 8
CAP = 192
CAPO = 64
AGG = 192
LANES = 128
PER_TILE = 4
PAD = 160
PIECE = 32
QUAD = 4
WIDE = 3 * PAD
F32 = jnp.float32
BF16 = jnp.bfloat16
HIGHEST = lax.Precision.HIGHEST
MESH = pl.DeviceIdType.MESH


def iota(shape, dim):
    return lax.broadcasted_iota(jnp.int32, shape, dim)


def halves(x):
    high = x.astype(BF16)
    return high, (x - high.astype(F32)).astype(BF16)


def stacked_left(x, block, width):
    rows, lanes = x.shape
    if lanes < width:
        x = jnp.concatenate([x, jnp.zeros((rows, width - lanes), F32)], 1)
    high = x.astype(BF16).astype(F32)
    low = x - high
    return (high + pltpu.roll(high, block, 1) + pltpu.roll(low, 2 * block, 1)).astype(BF16)


def stacked_right(x):
    high, low = halves(x)
    return jnp.concatenate([high, low, high], 0)


def dot(a, b):
    return jnp.dot(a, b, preferred_element_type=F32)


def nt(a, b, precision=None):
    return lax.dot_general(
        a, b, (((1,), (1,)), ((), ())), precision=precision, preferred_element_type=F32
    )


def kernel(
    blocks, subs,
    partner_hbm, counts_hbm, owner_hbm,
    rhs_hbm, coeff_hbm, s_ref_hbm, m_inv_hbm, restriction_hbm, c_inv_hbm,
    out, lift_out,
    partner_s, counts_s, owner_s, coeff, s_ref, m_inv, restriction, rpad,
    rhs, split, c_inv, lhs, lhs_s, left_m, left_s, field, resid, tall,
    msg1, msg3, got1, got3, y_a, y_b, got_a, got_b, edge, got_edge,
    face_msg, faces, pass_msg, passed, ends,
    s1, r1, s2, r2, s3, r3, s4, r4, sx, rx, sf, rf, se, re, sp, rp, load, load_c, load_s,
):
    elements = rhs.shape[1]
    trace = m_inv.shape[0]
    nrb = elements // AGG
    width = PER_TILE * AGG
    tiles = elements // width
    packs = blocks * nrb // LANES
    per_pack = LANES // nrb
    edge_lanes = edge.shape[1]
    me = lax.axis_index("blk")
    sub = lax.axis_index("sub")
    has_below = (sub > 0).astype(jnp.int32)
    has_above = (sub < subs - 1).astype(jnp.int32)
    rising = (me * 2 < blocks).astype(jnp.int32)

    def every(j):
        return rising * (blocks - 1 - j) + (1 - rising) * j

    def other(j):
        down = blocks - 1 - j
        down = down - (down <= me).astype(jnp.int32)
        up = j + (j >= me).astype(jnp.int32)
        return rising * down + (1 - rising) * up

    barrier = pltpu.get_barrier_semaphore()

    def greet(j, carry):
        pl.semaphore_signal(barrier, inc=1, device_id={"blk": other(j)}, device_id_type=MESH)
        return carry

    lax.fori_loop(0, blocks - 1, greet, 0)

    @pl.when(sub > 0)
    def _():
        pl.semaphore_signal(barrier, inc=1, device_id={"sub": sub - 1}, device_id_type=MESH)

    @pl.when(sub < subs - 1)
    def _():
        pl.semaphore_signal(barrier, inc=1, device_id={"sub": sub + 1}, device_id_type=MESH)

    small = [
        pltpu.make_async_copy(src, dst, load_s.at[i])
        for i, (src, dst) in enumerate(
            [
                (restriction_hbm, restriction), (owner_hbm, owner_s),
                (partner_hbm, partner_s), (counts_hbm, counts_s), (coeff_hbm, coeff),
                (m_inv_hbm, m_inv), (s_ref_hbm, s_ref),
            ]
        )
    ]
    loads = [
        pltpu.make_async_copy(
            rhs_hbm.at[:, pl.ds(t * width, width)],
            rhs.at[:, pl.ds(t * width, width)], load.at[t],
        )
        for t in range(tiles)
    ]
    load_solver = pltpu.make_async_copy(c_inv_hbm, c_inv, load_c)
    for copy in small[:5] + loads + small[5:]:
        copy.start()
    load_solver.start()

    def spread(src, dst, send, recv):
        def one(j, carry):
            peer = other(j)
            pltpu.make_async_remote_copy(
                src_ref=src, dst_ref=dst.at[me], send_sem=send.at[peer], recv_sem=recv.at[me],
                device_id={"blk": peer}, device_id_type=MESH,
            ).start()
            return carry

        lax.fori_loop(0, blocks - 1, one, 0)

    def handle(src, dst, send, recv, peer):
        return pltpu.make_async_remote_copy(
            src_ref=src, dst_ref=dst.at[peer], send_sem=send.at[peer], recv_sem=recv.at[peer],
            device_id={"blk": peer}, device_id_type=MESH,
        )

    def collect(src, dst, send, recv):
        def one(j, carry):
            handle(src, dst, send, recv, lax.rem(me + j, blocks)).wait_recv()
            return carry

        lax.fori_loop(1, blocks, one, 0)

    def sent(src, dst, send, recv):
        def one(j, carry):
            handle(src, dst, send, recv, lax.rem(me + j, blocks)).wait_send()
            return carry

        lax.fori_loop(1, blocks, one, 0)

    def beside(src, dst, slot, send, recv, peer):
        return pltpu.make_async_remote_copy(
            src_ref=src, dst_ref=dst.at[slot], send_sem=send.at[slot], recv_sem=recv.at[slot],
            device_id={"sub": peer}, device_id_type=MESH,
        )

    def edge_copy(slot, place_at, peer, peer_sub):
        return pltpu.make_async_remote_copy(
            src_ref=edge, dst_ref=got_edge.at[slot, place_at],
            send_sem=sx.at[slot, peer], recv_sem=rx.at[slot, place_at],
            device_id={"blk": peer, "sub": peer_sub}, device_id_type=MESH,
        )

    lane = iota((COARSE, LANES), 1)
    left_half = lane < LANES // 2
    zero_tile = jnp.zeros((COARSE, LANES), F32)

    def lane_sums(values, total, tile):
        for p in range(PER_TILE // 2):
            first, mid, last = (
                values[:, (3 * p + q) * LANES : (3 * p + q + 1) * LANES] for q in range(3)
            )
            even = first + jnp.where(left_half, mid, 0.0)
            odd = last + jnp.where(left_half, 0.0, mid)
            at = tile * PER_TILE + 2 * p
            total = jnp.where(lane == at, jnp.sum(even, 1, keepdims=True), total)
            total = jnp.where(lane == at + 1, jnp.sum(odd, 1, keepdims=True), total)
        return total

    def lane_picks(values, total, tile, offset):
        for a in range(PER_TILE):
            at = a * AGG + offset
            total = jnp.where(lane == tile * PER_TILE + a, values[:, at : at + 1], total)
        return total

    rpad[...] = jnp.zeros((COARSE, 2 * LANES), F32)
    for row in (0, PAD):
        split[row + trace : row + PAD] = jnp.zeros((PAD - trace, width), BF16)
    resid[trace:PAD] = jnp.zeros((PAD - trace, width), F32)
    tall[trace:PAD] = jnp.zeros((PAD - trace, LANES), F32)
    small[0].wait()
    r_lane = iota((COARSE, 2 * LANES), 1)
    rpad[:, 0:trace] = restriction[...]
    spread_r = rpad[...]
    left_r = stacked_left(spread_r, PAD, 4 * LANES)[:, :WIDE]

    row8 = iota((COARSE, LANES), 0)

    def place(values):
        values = jnp.where(lane < nrb, values, 0.0)
        return pltpu.roll(values, lax.rem(me, per_pack) * nrb, 1)

    def split_tile(cols):
        high, low = halves(rhs[:, cols])
        split[0:trace] = high
        split[PAD : PAD + trace] = low
        high = split[0:PAD]
        return jnp.concatenate([high, split[PAD : 2 * PAD], high], 0)

    def describe():
        coeff_sums = zero_tile
        for tile in range(tiles):
            c_row = jnp.broadcast_to(coeff[:, tile * width : (tile + 1) * width], (COARSE, width))
            coeff_sums = lane_sums(c_row, coeff_sums, tile)
        owner_tile = zero_tile
        for g in range(nrb):
            owner_tile = jnp.where(lane == g, owner_s[0, g].astype(F32), owner_tile)
        for k in range(4):
            owner_tile = jnp.where(
                (row8 == 1) & (lane == k), partner_s[0, k].astype(F32), owner_tile
            )
            owner_tile = jnp.where(
                (row8 == 2) & (lane == k), counts_s[0, k].astype(F32), owner_tile
            )
        owner_tile = jnp.where(row8 == 3, coeff_sums, owner_tile)
        msg1[8:16] = place(owner_tile)

    tall_lane = iota((trace, LANES), 1)
    tall_left = tall_lane < LANES // 2
    totals = jnp.zeros((trace, LANES), F32)
    for tile in range(tiles):
        loads[tile].wait()
        for p in range(PER_TILE // 2):
            first, mid, last = (
                rhs[:, tile * width + (3 * p + q) * LANES : tile * width + (3 * p + q + 1) * LANES]
                for q in range(3)
            )
            even = first + jnp.where(tall_left, mid, 0.0)
            odd = last + jnp.where(tall_left, 0.0, mid)
            at = tile * PER_TILE + 2 * p
            totals = jnp.where(tall_lane == at, jnp.sum(even, 1, keepdims=True), totals)
            totals = jnp.where(tall_lane == at + 1, jnp.sum(odd, 1, keepdims=True), totals)
        if tile == max(tiles - 2, 0):
            for copy in small[1:5]:
                copy.wait()
            describe()
    tall[0:trace] = totals
    sums = dot(left_r, stacked_right(tall[...]))
    msg1[0:8] = place(sums)
    got1[me] = msg1[...]

    pl.semaphore_wait(barrier, blocks - 1 + has_below + has_above)
    spread(msg1, got1, s1, r1)

    backward = pltpu.roll(spread_r, 2 * LANES - FACE, 1)
    forward = pltpu.roll(spread_r, FACE, 1)

    def at_slot(slot, from_slot):
        moved = backward if from_slot > slot else forward
        inside = (r_lane >= slot * FACE) & (r_lane < (slot + 1) * FACE)
        return jnp.where(inside, moved, 0.0)

    low_part, high_part = at_slot(4, 5), at_slot(5, 4)
    sides = [at_slot(k, k ^ 1) for k in range(4)]
    for copy in small[5:]:
        copy.wait()
    for ref, src in ((lhs, m_inv), (lhs_s, s_ref)):
        ref[...] = jnp.zeros((PAD, 2 * LANES), F32)
        ref[0:trace, 0:trace] = src[...]
    left_m[0:PAD] = stacked_left(lhs[...], PAD, 4 * LANES)
    base = jnp.concatenate(
        [dot(left_r, stacked_right(lhs_s[...]))]
        + [spread_r - low_part - high_part, low_part, high_part] + sides,
        0,
    )
    moved = dot(stacked_left(base, PAD, 4 * LANES)[:, :WIDE], stacked_right(lhs[...]))
    left_m[PAD : PAD + 8 * COARSE] = stacked_left(moved, PAD, 4 * LANES)
    lhs[152:160] = spread_r

    groups = blocks // QUAD
    group = me // QUAD
    spot = lax.rem(me, QUAD)

    def face_copy(place_at, to, rows=slice(None)):
        return pltpu.make_async_remote_copy(
            src_ref=face_msg.at[rows], dst_ref=faces.at[place_at, rows], send_sem=sf.at[to],
            recv_sem=rf.at[place_at], device_id={"blk": group * QUAD + to}, device_id_type=MESH,
        )

    def pass_copy(place_at, to):
        return pltpu.make_async_remote_copy(
            src_ref=pass_msg.at[to], dst_ref=passed.at[place_at], send_sem=sp.at[to],
            recv_sem=rp.at[place_at], device_id={"blk": to * QUAD + spot}, device_id_type=MESH,
        )

    queue = [(step, piece) for piece in range(160 // PIECE) for step in range(1, QUAD)]

    def pace(count):
        for _ in range(min(count, len(queue))):
            step, piece = queue.pop(0)
            rows = pl.ds(piece * PIECE, PIECE)
            face_copy(spot, lax.rem(spot + step, QUAD), rows).start()

    first_src = field.at[96:152, LANES : 2 * LANES]
    last_src = field.at[96:152, elements : elements + LANES]

    less = zero_tile
    firsts = zero_tile
    lasts = zero_tile
    side_sums = zero_tile
    for tile in [0, tiles - 1] + list(range(1, tiles - 1)):
        cols = slice(tile * width, (tile + 1) * width)
        rows = PAD + (8 if tile == 0 else 4) * COARSE
        made = dot(left_m[0:rows, 0:WIDE], split_tile(cols))
        scale = 0.5 / coeff[:, cols]
        field[:, LANES + tile * width : LANES + (tile + 1) * width] = made[:PAD] * scale
        parts = [made[PAD + 8 * i : PAD + 8 * i + 8] for i in range((rows - PAD) // COARSE)]
        less = lane_sums(0.5 * parts[0] + parts[1] * scale, less, tile)
        firsts = lane_picks(parts[2] * scale, firsts, tile, 0)
        lasts = lane_picks(parts[3] * scale, lasts, tile, AGG - 1)
        if tile == 0:
            side_lane = iota((COARSE, 2 * LANES), 1)
            for k in range(4):
                part = parts[4 + k][:, : 2 * LANES] * scale[:, : 2 * LANES]
                part = jnp.where(side_lane < counts_s[0, k], part, 0.0)
                side_sums = jnp.where(lane == k, jnp.sum(part, 1, keepdims=True), side_sums)
            head = field[0:104, LANES : 2 * LANES]
            tail = field[0:104, 2 * LANES : 3 * LANES]
            half = iota((56, LANES), 1) < LANES // 2
            turned = pltpu.roll(tail, LANES // 2, 1)
            upper = jnp.concatenate([turned[56:104], jnp.zeros((8, LANES), F32)], 0)
            face_msg[0:104] = head
            face_msg[104:160] = jnp.where(half, tail[0:56], upper)
            faces[spot] = face_msg[...]

            @pl.when(sub > 0)
            def _():
                beside(first_src, ends, 1, se, re, sub - 1).start()

        if tile == tiles - 1:

            @pl.when(sub < subs - 1)
            def _():
                beside(last_src, ends, 0, se, re, sub + 1).start()

        pace(3)

    left_s[...] = stacked_left(lhs_s[...], PAD, 4 * LANES)
    row56 = iota((56, width), 0)

    def second(tile):
        cols = slice(tile * width, (tile + 1) * width)
        u = field[:, LANES + tile * width : LANES + (tile + 1) * width]
        su = dot(left_s[:, 0:WIDE], stacked_right(u))
        c_row = coeff[:, cols]
        resid[0:trace] = rhs[:, cols] - su[:trace] * c_row - u[:trace]
        wide = field[96:152, tile * width : (tile + 1) * width + 2 * LANES]
        span = width + 2 * LANES
        below = pltpu.roll(wide, 1, 1)[:, LANES : LANES + width]
        above = pltpu.roll(wide, span - 1, 1)[:, LANES : LANES + width]
        below = pltpu.roll(below, 56 - FACE, 0)
        above = pltpu.roll(above, FACE, 0)
        column = jnp.where(
            (row56 >= 4) & (row56 < 4 + FACE), below,
            jnp.where((row56 >= 4 + FACE) & (row56 < 4 + 2 * FACE), above, 0.0),
        )
        resid[96:152] = resid[96:152] + column
        made = dot(left_m[0:PAD, 0:WIDE], stacked_right(resid[...]))
        out[:, cols] = u[:trace] + made[:trace] * (0.5 / c_row)

    early = [1] if tiles > 2 else []
    for tile in early:
        second(tile)
        pace(len(queue))

    @pl.when(sub > 0)
    def _():
        beside(last_src, ends, 0, se, re, sub - 1).wait_recv()
        field[96:152, 0:LANES] = ends[0]

    @pl.when(sub == 0)
    def _():
        field[96:152, 0:LANES] = jnp.zeros((56, LANES), F32)

    @pl.when(sub < subs - 1)
    def _():
        beside(first_src, ends, 1, se, re, sub + 1).wait_recv()
        field[96:152, LANES + elements : 2 * LANES + elements] = ends[1]

    @pl.when(sub == subs - 1)
    def _():
        field[96:152, LANES + elements : 2 * LANES + elements] = jnp.zeros((56, LANES), F32)

    ends_left = pltpu.roll(
        jnp.concatenate([low_part, high_part], 0), 2 * LANES - 96, 1
    )[:, :56]
    from_ends = jnp.dot(
        ends_left,
        jnp.concatenate(
            [field[96:152, 0:LANES], field[96:152, LANES + elements : 2 * LANES + elements]], 1
        ),
        precision=HIGHEST, preferred_element_type=F32,
    )
    below_last = from_ends[8:16, LANES - 1 : LANES]
    above_first = from_ends[0:8, LANES : LANES + 1]
    next_first = jnp.where(
        lane == nrb - 1, above_first, pltpu.roll(firsts, LANES - 1, 1)
    )
    last_before = jnp.where(lane == 0, below_last, pltpu.roll(lasts, 1, 1))
    msg3[0:8] = place(sums - less - firsts + next_first - lasts + last_before)
    msg3[8:16] = place(side_sums)
    got3[me] = msg3[...]
    spread(msg3, got3, s3, r3)

    collect(msg1, got1, s1, r1)

    def packed(got):
        return [
            jnp.sum(got[t * per_pack : (t + 1) * per_pack], 0) for t in range(packs)
        ]

    first_pack = packed(got1)
    owner_rows = [p[8:9] for p in first_pack]
    eye = iota((LANES, LANES), 0) == iota((LANES, LANES), 1)
    earlier = iota((LANES, LANES), 0) < iota((LANES, LANES), 1)
    owner_cols = [
        jnp.sum(jnp.where(eye, row, 0.0), 1, keepdims=True) for row in owner_rows
    ]
    slot_rows = []
    for t in range(packs):
        slot = jnp.zeros((1, LANES), F32)
        for before in range(t + 1):
            same = owner_cols[before] == owner_rows[t]
            if before == t:
                same = same & earlier
            slot = slot + jnp.sum(jnp.where(same, 1.0, 0.0), 0, keepdims=True)
        slot_rows.append(slot)
    order = COARSE * CAPO
    slot_of = (iota((order, LANES), 0) // COARSE).astype(F32)
    me_real = me.astype(F32)
    chosen = [
        jnp.where((slot_of == slot_rows[t]) & (owner_rows[t] == me_real), 1.0, 0.0).astype(BF16)
        for t in range(packs)
    ]
    pick = lax.rem(iota((order, 2 * COARSE), 0), COARSE) == lax.rem(
        iota((order, 2 * COARSE), 1), COARSE
    )

    def solve(packs_of):
        total = jnp.zeros((order, 2 * COARSE), F32)
        for t in range(packs):
            total = total + nt(chosen[t], jnp.concatenate(halves(packs_of[t]), 0))
        column = jnp.sum(jnp.where(pick, total, 0.0), 1, keepdims=True)
        return jnp.sum(c_inv[...] * column, 0, keepdims=True)

    load_solver.wait()
    y_a[...] = solve([p[0:8] for p in first_pack])
    got_a[me] = y_a[...]
    in_block = lax.rem(lane, nrb)
    keep_eight = iota((COARSE, order), 0) == lax.rem(iota((COARSE, order), 1), COARSE)
    mine = jnp.concatenate(halves(jnp.where(keep_eight, 0.5 * y_a[...], 0.0)), 0)
    for t in range(packs):
        held = dot(mine, chosen[t])
        held = held[0:8] + held[8:16]
        turned = pltpu.roll(
            jnp.where(in_block == nrb - 1, held, 0.0), LANES - (nrb - 1), 1,
            stride=1, stride_axis=0,
        ) + pltpu.roll(jnp.where(in_block == 0, held, 0.0), COARSE, 1, stride=1, stride_axis=0)
        edge[:, t * LANES : (t + 1) * LANES] = jnp.sum(turned, 0, keepdims=True)

    def send_edges(slot, peer_sub):
        def one(j, carry):
            edge_copy(slot, me, every(j), peer_sub).start()
            return carry

        lax.fori_loop(0, blocks, one, 0)

    @pl.when(sub < subs - 1)
    def _():
        send_edges(0, sub + 1)

    @pl.when(sub > 0)
    def _():
        send_edges(1, sub - 1)

    spread(y_a, got_a, s2, r2)

    for tile in range(tiles):
        if tile not in early:
            second(tile)

    unit = jnp.where(iota((PAD, trace), 0) == iota((PAD, trace), 1), 1.0, 0.0)
    r_high = restriction_high = spread_r[:, :trace].astype(BF16).astype(F32)
    r_low = spread_r[:, :trace] - restriction_high
    left_lift = nt(
        unit.astype(BF16), jnp.concatenate([r_high, r_high, r_low], 0).astype(BF16)
    )
    lifted = nt(
        unit.astype(BF16),
        jnp.concatenate([r_high, jnp.zeros((15 * COARSE, trace), F32)], 0).astype(BF16),
    ) + nt(
        unit.astype(BF16),
        jnp.concatenate([r_low, jnp.zeros((15 * COARSE, trace), F32)], 0).astype(BF16),
    )
    left_lift = left_lift.astype(BF16)
    both = lhs[...]
    weights = nt(
        both[:, :trace],
        jnp.concatenate([base[:, :trace], jnp.zeros((8 * COARSE, trace), F32)], 0), HIGHEST,
    )
    signs = jnp.where(iota((PAD, LANES), 1) < 4 * COARSE, -0.5, 0.5)
    rows_in = iota((PAD, LANES), 0) < trace
    correct = jnp.where(rows_in, lifted + weights * signs, 0.0)
    left_wide = stacked_left(correct, 8 * COARSE, 2 * LANES)[:, : 24 * COARSE]
    left_slim = stacked_left(
        jnp.where(iota((PAD, LANES), 1) < 4 * COARSE, correct, 0.0), 4 * COARSE, LANES
    )[:, : 12 * COARSE]
    left_reduced = stacked_left(weights[152:160], 8 * COARSE, 2 * LANES)[:, : 24 * COARSE]

    target = jnp.where(lane < nrb, me * nrb + lane, -1)
    for k in range(4):
        target = jnp.where(lane == nrb + k, partner_s[0, k] * nrb, target)
    pairs = [
        jnp.where(row8 == 0, owner_rows[t] + 1.0, slot_rows[t]).astype(BF16)
        for t in range(packs)
    ]
    own_sel = []
    found = zero_tile
    for t in range(packs):
        sel = iota((LANES, LANES), 0) + t * LANES == target[0:1]
        own_sel.append(jnp.where(sel, 1.0, 0.0).astype(BF16))
        found = found + dot(pairs[t], own_sel[t])
    back_owner, back_slot = found[0:1], found[1:2]
    back = jnp.where(slot_of == back_slot, 1.0, 0.0).astype(BF16)

    lane_row = iota((LANES, LANES), 0)
    def cross(values, extra):
        rows = values[0].shape[0]
        results = []
        for t in range(packs):
            wanted = first_pack[t][9:10] * float(nrb) + extra
            total = jnp.zeros((rows, LANES), F32)
            for source in range(packs):
                sel = (lane_row + source * LANES).astype(F32) == wanted
                total = total + dot(values[source], jnp.where(sel, 1.0, 0.0).astype(BF16))
            results.append(total)
        return results

    crossed_pairs = cross(pairs, 0.0)
    slots_both = [
        jnp.concatenate(
            [
                jnp.where(slot_of == slot_rows[t], 1.0, 0.0),
                jnp.where(slot_of == crossed_pairs[t][1:2], 1.0, 0.0),
            ],
            1,
        ).astype(BF16)
        for t in range(packs)
    ]
    owners_both = [
        jnp.concatenate([owner_rows[t] + 1.0, crossed_pairs[t][0:1]], 1) for t in range(packs)
    ]
    keep_row = (
        iota((blocks, COARSE, order), 1) == lax.rem(iota((blocks, COARSE, order), 2), COARSE)
    )

    def rows_of(got):
        rows = jnp.where(keep_row, got[...], 0.0).reshape(blocks * COARSE, order)
        return jnp.concatenate(halves(rows), 0)

    def fetch(rows, at_slot, owner_row):
        lanes = at_slot.shape[1]
        block_of = iota((blocks, COARSE, lanes), 0).astype(F32) + 1.0
        made = dot(rows, at_slot)
        count = blocks * COARSE
        made = (made[:count] + made[count:]).reshape(blocks, COARSE, lanes)
        return jnp.sum(jnp.where(block_of == owner_row[None], made, 0.0), 0)

    def fold(values):
        total = values
        for k in range(1, 4):
            total = total + pltpu.roll(values, LANES - k, 1)
        return jnp.where(in_block == 0, total, 0.0)

    packed_row = iota((160, LANES), 0)
    face_row = jnp.where(
        packed_row < 104, packed_row,
        jnp.where(iota((160, LANES), 1) < LANES // 2, packed_row - 104, packed_row - 48),
    )

    def sources(of):
        wanted = jnp.full((160, LANES), -1.0, F32)
        for q in range(4):
            inside = (face_row >= q * FACE) & (face_row < (q + 1) * FACE)
            wanted = jnp.where(inside, of[q ^ 1], wanted)
        return wanted

    first_block = (group * QUAD).astype(F32)

    def from_group(wanted):
        taken = jnp.zeros((160, LANES), F32)
        for q in range(QUAD):
            taken = jnp.where(wanted == first_block + float(q), faces[q], taken)
        return taken

    for step in range(1, QUAD):
        whence = lax.rem(spot + step, QUAD)
        face_copy(whence, whence).wait_recv()
    for step in range(1, groups):
        to = lax.rem(group + step, groups)
        wanted = []
        for k in range(4):
            total = jnp.zeros((1, 1), F32)
            for t in range(packs):
                here = lane[0:1] + t * LANES == (to * QUAD + spot) * nrb + k
                total = total + jnp.sum(
                    jnp.where(here, first_pack[t][9:10], 0.0), 1, keepdims=True
                )
            wanted.append(total)
        pass_msg[to] = from_group(sources(wanted))
        pass_copy(group, to).start()

    collect(msg3, got3, s3, r3)
    third_pack = packed(got3)
    swapped = (in_block + 1 - 2 * lax.rem(in_block, 2)).astype(F32)[0:1]
    side_in = cross([jnp.concatenate(halves(p[8:16]), 0) for p in third_pack], swapped)
    base_sums = [
        third_pack[t][0:8] + fold(side_in[t][0:8] + side_in[t][8:16]) for t in range(packs)
    ]

    collect(y_a, got_a, s2, r2)
    rows = rows_of(got_a)
    fetched = [0.5 * fetch(rows, slots_both[t], owners_both[t]) for t in range(packs)]

    def take_edges(slot, peer_sub):
        def one(j, carry):
            edge_copy(slot, lax.rem(me + j, blocks), lax.rem(me + j, blocks), peer_sub).wait_recv()
            return carry

        lax.fori_loop(0, blocks, one, 0)

    @pl.when(sub > 0)
    def _():
        take_edges(0, sub - 1)

    @pl.when(sub == 0)
    def _():
        got_edge[0] = jnp.zeros((blocks, 1, edge_lanes), F32)

    @pl.when(sub < subs - 1)
    def _():
        take_edges(1, sub + 1)

    @pl.when(sub == subs - 1)
    def _():
        got_edge[1] = jnp.zeros((blocks, 1, edge_lanes), F32)

    near = [jnp.sum(got_edge[q], 0) for q in range(2)]
    states = []
    seconds = []
    for t in range(packs):
        omega, crossed = fetched[t][:, :LANES], fetched[t][:, LANES:]
        below, above = (
            jnp.broadcast_to(v[:, t * LANES : (t + 1) * LANES], (COARSE, LANES)) for v in near
        )
        beyond = jnp.where(in_block < COARSE, below, above)
        beyond = jnp.where(lax.rem(in_block, COARSE) == row8, beyond, 0.0)
        for bit in (1, 2, 4):
            beyond = jnp.where((row8 & bit) > 0, pltpu.roll(beyond, LANES - bit, 1), beyond)
        before = jnp.where(in_block == 0, beyond, pltpu.roll(omega, 1, 1))
        after = jnp.where(
            in_block == nrb - 1, pltpu.roll(beyond, nrb - 1 - COARSE, 1),
            pltpu.roll(omega, LANES - 1, 1),
        )
        step_down = omega - before
        step_up = omega - after
        values = [omega * first_pack[t][11:12], float(AGG) * omega, step_down, step_up]
        share = crossed * (-first_pack[t][10:11])
        for k in range(4):
            turned = share if k == 0 else pltpu.roll(share, LANES - k, 1)
            values.append(jnp.where(in_block == 0, turned, 0.0))
        change = dot(left_reduced, stacked_right(jnp.concatenate(values, 0)))
        seconds.append(base_sums[t] - change)
        states.append(jnp.concatenate([omega, step_down, step_up, zero_tile], 0))
    y_b[...] = solve(seconds)
    got_b[me] = y_b[...]
    spread(y_b, got_b, s4, r4)

    state = jnp.zeros((8 * COARSE, LANES), F32)
    for t in range(packs):
        state = state + dot(jnp.concatenate(halves(states[t]), 0), own_sel[t])
    state = state[0:32] + state[32:64]
    omega, step_down, step_up = state[0:8], state[8:16], state[16:24]
    across = [omega[:, nrb + k : nrb + k + 1] for k in range(4)]

    left_lateral = jnp.where(iota((PAD, LANES), 1) < 4 * FACE, lhs[:, 0:LANES], 0.0)
    left_lateral = jnp.where(iota((PAD, LANES), 0) < trace, left_lateral, 0.0)
    high, low = halves(left_lateral)
    left_lateral = jnp.concatenate([high, high, low], 1)

    def lateral_change():
        wanted = sources([partner_s[0, k].astype(F32) for k in range(4)])
        taken = from_group(wanted)
        for step in range(1, groups):
            whence = lax.rem(group + step, groups)
            pass_copy(whence, whence).wait_recv()
            start = (whence * QUAD).astype(F32)
            inside = (wanted >= start) & (wanted < start + float(QUAD))
            taken = jnp.where(inside, passed[whence], taken)
        unfolded = taken[104:160]
        turned = pltpu.roll(unfolded, LANES // 2, 1)
        wide = jnp.concatenate(
            [taken[0:104], jnp.concatenate([unfolded, turned[0:48]], 0)], 1
        )
        backward = pltpu.roll(wide, 104 - FACE, 0)
        forward = pltpu.roll(wide, FACE, 0)
        row = iota((104, 2 * LANES), 0)
        col = iota((104, 2 * LANES), 1)
        lateral = jnp.zeros((104, 2 * LANES), F32)
        for k in range(4):
            inside = (row >= k * FACE) & (row < (k + 1) * FACE) & (col < counts_s[0, k])
            lateral = jnp.where(inside, backward if k % 2 == 0 else forward, lateral)
        lateral = jnp.concatenate([lateral, jnp.zeros((LANES - 104, 2 * LANES), F32)], 0)
        made = dot(left_lateral, stacked_right(lateral))
        out[:, 0 : 2 * LANES] = out[:, 0 : 2 * LANES] + made[:trace] * (
            0.5 / coeff[:, 0 : 2 * LANES]
        )

    wide_lane = iota((COARSE, width), 1)
    step = lax.rem(wide_lane, AGG)

    def spread_lanes(values, tile):
        pieces = []
        for p in range(PER_TILE // 2):
            at = tile * PER_TILE + 2 * p
            even = jnp.broadcast_to(values[:, at : at + 1], (COARSE, LANES))
            odd = jnp.broadcast_to(values[:, at + 1 : at + 2], (COARSE, LANES))
            pieces += [even, jnp.where(left_half, even, odd), odd]
        return jnp.concatenate(pieces, 1)

    def coarse_change(tile):
        cols = slice(tile * width, (tile + 1) * width)
        inverse = 1.0 / coeff[:, cols]
        here = spread_lanes(omega, tile)
        scaled = here * inverse
        down = jnp.where(step == 0, spread_lanes(step_down, tile) * inverse, 0.0)
        up = jnp.where(step == AGG - 1, spread_lanes(step_up, tile) * inverse, 0.0)
        rows = [here, scaled, down, up]
        if tile == 0:
            for k in range(4):
                rows.append(jnp.where(wide_lane < counts_s[0, k], across[k] * inverse, 0.0))
        left = left_wide if tile == 0 else left_slim
        made = dot(left, stacked_right(jnp.concatenate(rows, 0)))
        out[:, cols] = out[:, cols] + made[:trace]

    for tile in range(tiles):
        coarse_change(tile)
    sent(msg1, got1, s1, r1)
    for step in range(1, QUAD):
        face_copy(spot, lax.rem(spot + step, QUAD)).wait_send()
    sent(y_a, got_a, s2, r2)
    sent(msg3, got3, s3, r3)

    def edges_sent(slot, peer_sub):
        def one(j, carry):
            edge_copy(slot, me, lax.rem(me + j, blocks), peer_sub).wait_send()
            return carry

        lax.fori_loop(0, blocks, one, 0)

    @pl.when(sub < subs - 1)
    def _():
        beside(last_src, ends, 0, se, re, sub + 1).wait_send()
        edges_sent(0, sub + 1)

    @pl.when(sub > 0)
    def _():
        beside(first_src, ends, 1, se, re, sub - 1).wait_send()
        edges_sent(1, sub - 1)

    lateral_change()
    for step in range(1, groups):
        pass_copy(group, lax.rem(group + step, groups)).wait_send()

    collect(y_b, got_b, s4, r4)
    final = 0.5 * fetch(rows_of(got_b), back, back_owner)
    high = final.astype(BF16).astype(F32)
    lift_out[...] = dot(
        left_lift, jnp.concatenate([high, final - high, high], 0).astype(BF16)
    )[: lift_out.shape[0]]
    sent(y_b, got_b, s4, r4)


def finish(lift, held, out_hbm, done, store):
    rows, elements = held.shape
    width = 2 * AGG
    tiles = elements // width
    stores = []
    for t in range(tiles):
        cols = pl.ds(t * width, width)
        stores.append(pltpu.make_async_copy(done.at[:, cols], out_hbm.at[:, cols], store.at[t]))
    split = iota((rows, LANES), 1) < LANES // 2
    for t in range(tiles):
        first = jnp.broadcast_to(lift[:rows, 2 * t : 2 * t + 1], (rows, LANES))
        second = jnp.broadcast_to(lift[:rows, 2 * t + 1 : 2 * t + 2], (rows, LANES))
        left, mid, right = (pl.ds(t * width + q * LANES, LANES) for q in range(3))
        done[:, left] = held[:, left] + first
        done[:, mid] = held[:, mid] + jnp.where(split, first, second)
        done[:, right] = held[:, right] + second
        stores[t].start()
    for copy in stores:
        copy.wait()


def per_device(blocks, subs, rhs, coeff, s_ref, m_inv, restriction, partner, counts, owner, c_inv):
    trace, elements = rhs.shape
    width = PER_TILE * AGG
    order = COARSE * CAPO
    vmem = pl.BlockSpec(memory_space=pltpu.VMEM)
    edge_lanes = blocks * owner.shape[2]
    far = pl.BlockSpec(memory_space=pltpu.HBM)
    dma = pltpu.SemaphoreType.DMA
    held, lift = pl.pallas_call(
        functools.partial(kernel, blocks, subs),
        out_shape=(
            pltpu.VMEM((trace, elements), F32),
            pltpu.VMEM((152, LANES), F32),
        ),
        in_specs=[far] * 9,
        out_specs=(vmem, vmem),
        scratch_shapes=[
            pltpu.SMEM((1, 4), jnp.int32),
            pltpu.SMEM((1, 4), jnp.int32),
            pltpu.SMEM((1, owner.shape[2]), jnp.int32),
            pltpu.VMEM((1, elements), F32),
            pltpu.VMEM((trace, trace), F32),
            pltpu.VMEM((trace, trace), F32),
            pltpu.VMEM((COARSE, trace), F32),
            pltpu.VMEM((COARSE, 2 * LANES), F32),
            pltpu.VMEM((trace, elements), F32),
            pltpu.VMEM((2 * PAD, width), BF16),
            pltpu.VMEM((order, order), F32),
            pltpu.VMEM((PAD, 2 * LANES), F32),
            pltpu.VMEM((PAD, 2 * LANES), F32),
            pltpu.VMEM((PAD + 8 * COARSE, 4 * LANES), BF16),
            pltpu.VMEM((PAD, 4 * LANES), BF16),
            pltpu.VMEM((PAD, elements + 2 * LANES), F32),
            pltpu.VMEM((PAD, width), F32),
            pltpu.VMEM((PAD, LANES), F32),
            pltpu.VMEM((16, LANES), F32),
            pltpu.VMEM((16, LANES), F32),
            pltpu.VMEM((blocks, 16, LANES), F32),
            pltpu.VMEM((blocks, 16, LANES), F32),
            pltpu.VMEM((1, order), F32),
            pltpu.VMEM((1, order), F32),
            pltpu.VMEM((blocks, 1, order), F32),
            pltpu.VMEM((blocks, 1, order), F32),
            pltpu.VMEM((1, edge_lanes), F32),
            pltpu.VMEM((2, blocks, 1, edge_lanes), F32),
            pltpu.VMEM((160, LANES), F32),
            pltpu.VMEM((QUAD, 160, LANES), F32),
            pltpu.VMEM((blocks // QUAD, 160, LANES), F32),
            pltpu.VMEM((blocks // QUAD, 160, LANES), F32),
            pltpu.VMEM((2, 56, LANES), F32),
        ]
        + [dma((blocks,))] * 8
        + [dma((2, blocks))] * 2
        + [dma((QUAD,))] * 2
        + [dma((2,))] * 2
        + [dma((blocks // QUAD,))] * 2
        + [dma((elements // width,)), dma, dma((7,))],
        compiler_params=pltpu.CompilerParams(
            collective_id=0, has_side_effects=True
        ),
    )(
        partner, counts[0], owner[0], rhs, coeff[None, :], s_ref, m_inv, restriction, c_inv[0, 0],
    )
    pairs = elements // (2 * AGG)
    return pl.pallas_call(
        finish,
        out_shape=jax.ShapeDtypeStruct((trace, elements), F32),
        in_specs=[vmem, vmem],
        out_specs=far,
        scratch_shapes=[
            pltpu.VMEM((trace, elements), F32),
            dma((pairs,)),
        ],
    )(*[pltpu.with_memory_space_constraint(v, pltpu.VMEM) for v in (lift, held)])


def solution(mesh):
    in_specs = (
        P(None, ("blk", "sub")),
        P(("blk", "sub")),
        P(),
        P(),
        P(),
        P("blk", None),
        P("blk", "sub", None),
        P("blk", "sub", None),
        P("blk", "sub", None, None),
    )
    out_specs = P(None, ("blk", "sub"))
    body = functools.partial(per_device, mesh.shape["blk"], mesh.shape["sub"])
    return jax.shard_map(
        body, mesh=mesh, in_specs=in_specs, out_specs=out_specs, check_vma=False
    )
```

time: 26.8 us -> 22.9 us (0.85)
  Pallas kernels: 26.7 us -> 22.7 us
    pallas_call x1, Pallas kernels: 25.3 us -> 21.3 us  [per_device(): pl.pallas_call(functools.partial(kernel, blocks, subs), out_shape=(pltpu....]
where the time goes in v2:
time: 22.9 us; the launch traced here: 22.7 us
  Pallas kernels  22.7 us (99%)
    pallas_call x1, Pallas kernels, per_device(): pl.pallas_call(functools.partial(kernel, blocks, subs), out_shape=(pltpu....  21.3 us
    pallas_call x1, Pallas kernels, per_device(): pl.pallas_call(finish, out_shape=jax.ShapeDtypeStruct((trace, elements),...  1.4 us

profile of v2, /device:TPU:0, one launch (start us, length us, event | category | flops | bytes accessed | tf_op | source)
XLA Modules:
  0.0 22.7 jit_solution(9027813459857547449)
XLA Ops:
  0.0 21.3 %shard_map.91 = (f32[150,3072]{1,0:T(8,128)S(1)}, f32[152,128]{1,0:T(8,128)S(1)}) custom-call(s32[1,4]{1,0:T(1,128)} %partner_hbm.1, s32[1,4]{1,0:T(1,128)} %bitcast.6, s32[1,16]{1,0:T(1,128)} %bitcast.7, f32[150,3072]{1,0:T(8,128)} %rhs_hbm.1, f32[1,3072]{1,0:T(1,128)} %bitcast.5, f32[150,150]{1,0:T(8,128)} %s_ref_hbm.1, f32[150,150]{1,0:T(8,128)} %m_inv_hbm.1, ...), custom_call_target="tpu_custom_call" | custom-call | tf_op jit(solution)/shard_map/pallas_call | solution.py:835
  21.3 1.4 %shard_map.92 = f32[150,3072]{1,0:T(8,128)} custom-call(f32[152,128]{1,0:T(8,128)S(1)} %get-tuple-element.7.lift, f32[150,3072]{1,0:T(8,128)S(1)} %get-tuple-element.8.held), custom_call_target="tpu_custom_call" | custom-call | tf_op jit(solution)/shard_map/pallas_call | solution.py:891

commit v3 on v2

--- a/solution.py
+++ b/solution.py
@@ -63,7 +63,7 @@
     rhs_hbm, coeff_hbm, s_ref_hbm, m_inv_hbm, restriction_hbm, c_inv_hbm,
     out, lift_out,
     partner_s, counts_s, owner_s, coeff, s_ref, m_inv, restriction, rpad,
-    rhs, split, c_inv, lhs, lhs_s, left_m, left_s, field, resid, tall,
+    rhs, split, c_inv, lhs, lhs_s, left_m, left_s, field, resid, tall, base,
     msg1, msg3, got1, got3, y_a, y_b, got_a, got_b, edge, got_edge,
     face_msg, faces, pass_msg, passed, ends,
     s1, r1, s2, r2, s3, r3, s4, r4, sx, rx, sf, rf, se, re, sp, rp, load, load_c, load_s,
@@ -131,34 +131,26 @@
 
     def spread(src, dst, send, recv):
         def one(j, carry):
-            peer = other(j)
             pltpu.make_async_remote_copy(
-                src_ref=src, dst_ref=dst.at[me], send_sem=send.at[peer], recv_sem=recv.at[me],
-                device_id={"blk": peer}, device_id_type=MESH,
+                src_ref=src, dst_ref=dst.at[me], send_sem=send, recv_sem=recv,
+                device_id={"blk": other(j)}, device_id_type=MESH,
             ).start()
             return carry
 
         lax.fori_loop(0, blocks - 1, one, 0)
 
-    def handle(src, dst, send, recv, peer):
+    def all_of(dst, send, recv):
+        part = dst.at[pl.ds(0, blocks - 1)]
         return pltpu.make_async_remote_copy(
-            src_ref=src, dst_ref=dst.at[peer], send_sem=send.at[peer], recv_sem=recv.at[peer],
-            device_id={"blk": peer}, device_id_type=MESH,
+            src_ref=part, dst_ref=part, send_sem=send, recv_sem=recv,
+            device_id={"blk": other(0)}, device_id_type=MESH,
         )
 
     def collect(src, dst, send, recv):
-        def one(j, carry):
-            handle(src, dst, send, recv, lax.rem(me + j, blocks)).wait_recv()
-            return carry
-
-        lax.fori_loop(1, blocks, one, 0)
+        all_of(dst, send, recv).wait_recv()
 
     def sent(src, dst, send, recv):
-        def one(j, carry):
-            handle(src, dst, send, recv, lax.rem(me + j, blocks)).wait_send()
-            return carry
-
-        lax.fori_loop(1, blocks, one, 0)
+        all_of(dst, send, recv).wait_send()
 
     def beside(src, dst, slot, send, recv, peer):
         return pltpu.make_async_remote_copy(
@@ -166,11 +158,16 @@
             device_id={"sub": peer}, device_id_type=MESH,
         )
 
-    def edge_copy(slot, place_at, peer, peer_sub):
+    def edge_copy(slot, peer, peer_sub):
         return pltpu.make_async_remote_copy(
-            src_ref=edge, dst_ref=got_edge.at[slot, place_at],
-            send_sem=sx.at[slot, peer], recv_sem=rx.at[slot, place_at],
-            device_id={"blk": peer, "sub": peer_sub}, device_id_type=MESH,
+            src_ref=edge, dst_ref=got_edge.at[slot, me], send_sem=sx.at[slot],
+            recv_sem=rx.at[slot], device_id={"blk": peer, "sub": peer_sub}, device_id_type=MESH,
+        )
+
+    def all_edges(slot, peer_sub):
+        return pltpu.make_async_remote_copy(
+            src_ref=got_edge.at[slot], dst_ref=got_edge.at[slot], send_sem=sx.at[slot],
+            recv_sem=rx.at[slot], device_id={"sub": peer_sub}, device_id_type=MESH,
         )
 
     lane = iota((COARSE, LANES), 1)
@@ -261,9 +258,6 @@
     msg1[0:8] = place(sums)
     got1[me] = msg1[...]
 
-    pl.semaphore_wait(barrier, blocks - 1 + has_below + has_above)
-    spread(msg1, got1, s1, r1)
-
     backward = pltpu.roll(spread_r, 2 * LANES - FACE, 1)
     forward = pltpu.roll(spread_r, FACE, 1)
 
@@ -274,20 +268,35 @@
 
     low_part, high_part = at_slot(4, 5), at_slot(5, 4)
     sides = [at_slot(k, k ^ 1) for k in range(4)]
-    for copy in small[5:]:
-        copy.wait()
-    for ref, src in ((lhs, m_inv), (lhs_s, s_ref)):
-        ref[...] = jnp.zeros((PAD, 2 * LANES), F32)
-        ref[0:trace, 0:trace] = src[...]
-    left_m[0:PAD] = stacked_left(lhs[...], PAD, 4 * LANES)
-    base = jnp.concatenate(
-        [dot(left_r, stacked_right(lhs_s[...]))]
-        + [spread_r - low_part - high_part, low_part, high_part] + sides,
-        0,
-    )
-    moved = dot(stacked_left(base, PAD, 4 * LANES)[:, :WIDE], stacked_right(lhs[...]))
-    left_m[PAD : PAD + 8 * COARSE] = stacked_left(moved, PAD, 4 * LANES)
-    lhs[152:160] = spread_r
+
+    def prepare():
+        for copy in small[5:]:
+            copy.wait()
+        for ref, src in ((lhs, m_inv), (lhs_s, s_ref)):
+            ref[...] = jnp.zeros((PAD, 2 * LANES), F32)
+            ref[0:trace, 0:trace] = src[...]
+        left_m[0:PAD] = stacked_left(lhs[...], PAD, 4 * LANES)
+        base[...] = jnp.concatenate(
+            [dot(left_r, stacked_right(lhs_s[...]))]
+            + [spread_r - low_part - high_part, low_part, high_part] + sides,
+            0,
+        )
+        moved = dot(stacked_left(base[...], PAD, 4 * LANES)[:, :WIDE], stacked_right(lhs[...]))
+        left_m[PAD : PAD + 8 * COARSE] = stacked_left(moved, PAD, 4 * LANES)
+        left_s[...] = stacked_left(lhs_s[...], PAD, 4 * LANES)
+        lhs[152:160] = spread_r
+
+    @pl.when(rising == 1)
+    def _():
+        prepare()
+
+
+    pl.semaphore_wait(barrier, blocks - 1 + has_below + has_above)
+    spread(msg1, got1, s1, r1)
+
+    @pl.when(rising == 0)
+    def _():
+        prepare()
 
     groups = blocks // QUAD
     group = me // QUAD
@@ -357,7 +366,6 @@
 
         pace(3)
 
-    left_s[...] = stacked_left(lhs_s[...], PAD, 4 * LANES)
     row56 = iota((56, width), 0)
 
     def second(tile):
@@ -385,44 +393,49 @@
         second(tile)
         pace(len(queue))
 
-    @pl.when(sub > 0)
-    def _():
-        beside(last_src, ends, 0, se, re, sub - 1).wait_recv()
-        field[96:152, 0:LANES] = ends[0]
-
-    @pl.when(sub == 0)
-    def _():
-        field[96:152, 0:LANES] = jnp.zeros((56, LANES), F32)
-
-    @pl.when(sub < subs - 1)
-    def _():
-        beside(first_src, ends, 1, se, re, sub + 1).wait_recv()
-        field[96:152, LANES + elements : 2 * LANES + elements] = ends[1]
-
-    @pl.when(sub == subs - 1)
-    def _():
-        field[96:152, LANES + elements : 2 * LANES + elements] = jnp.zeros((56, LANES), F32)
-
-    ends_left = pltpu.roll(
-        jnp.concatenate([low_part, high_part], 0), 2 * LANES - 96, 1
-    )[:, :56]
-    from_ends = jnp.dot(
-        ends_left,
-        jnp.concatenate(
-            [field[96:152, 0:LANES], field[96:152, LANES + elements : 2 * LANES + elements]], 1
-        ),
-        precision=HIGHEST, preferred_element_type=F32,
-    )
-    below_last = from_ends[8:16, LANES - 1 : LANES]
-    above_first = from_ends[0:8, LANES : LANES + 1]
-    next_first = jnp.where(
-        lane == nrb - 1, above_first, pltpu.roll(firsts, LANES - 1, 1)
-    )
-    last_before = jnp.where(lane == 0, below_last, pltpu.roll(lasts, 1, 1))
-    msg3[0:8] = place(sums - less - firsts + next_first - lasts + last_before)
-    msg3[8:16] = place(side_sums)
-    got3[me] = msg3[...]
-    spread(msg3, got3, s3, r3)
+    def send_third():
+        @pl.when(sub > 0)
+        def _():
+            beside(last_src, ends, 0, se, re, sub - 1).wait_recv()
+            field[96:152, 0:LANES] = ends[0]
+
+        @pl.when(sub == 0)
+        def _():
+            field[96:152, 0:LANES] = jnp.zeros((56, LANES), F32)
+
+        @pl.when(sub < subs - 1)
+        def _():
+            beside(first_src, ends, 1, se, re, sub + 1).wait_recv()
+            field[96:152, LANES + elements : 2 * LANES + elements] = ends[1]
+
+        @pl.when(sub == subs - 1)
+        def _():
+            field[96:152, LANES + elements : 2 * LANES + elements] = jnp.zeros((56, LANES), F32)
+
+        ends_left = pltpu.roll(
+            jnp.concatenate([low_part, high_part], 0), 2 * LANES - 96, 1
+        )[:, :56]
+        from_ends = jnp.dot(
+            ends_left,
+            jnp.concatenate(
+                [field[96:152, 0:LANES], field[96:152, LANES + elements : 2 * LANES + elements]], 1
+            ),
+            precision=HIGHEST, preferred_element_type=F32,
+        )
+        below_last = from_ends[8:16, LANES - 1 : LANES]
+        above_first = from_ends[0:8, LANES : LANES + 1]
+        next_first = jnp.where(
+            lane == nrb - 1, above_first, pltpu.roll(firsts, LANES - 1, 1)
+        )
+        last_before = jnp.where(lane == 0, below_last, pltpu.roll(lasts, 1, 1))
+        msg3[0:8] = place(sums - less - firsts + next_first - lasts + last_before)
+        msg3[8:16] = place(side_sums)
+        got3[me] = msg3[...]
+        spread(msg3, got3, s3, r3)
+
+    @pl.when(lax.rem(sub, 2) == 0)
+    def _():
+        send_third()
 
     collect(msg1, got1, s1, r1)
 
@@ -468,6 +481,8 @@
     load_solver.wait()
     y_a[...] = solve([p[0:8] for p in first_pack])
     got_a[me] = y_a[...]
+    spread(y_a, got_a, s2, r2)
+
     in_block = lax.rem(lane, nrb)
     keep_eight = iota((COARSE, order), 0) == lax.rem(iota((COARSE, order), 1), COARSE)
     mine = jnp.concatenate(halves(jnp.where(keep_eight, 0.5 * y_a[...], 0.0)), 0)
@@ -482,7 +497,7 @@
 
     def send_edges(slot, peer_sub):
         def one(j, carry):
-            edge_copy(slot, me, every(j), peer_sub).start()
+            edge_copy(slot, every(j), peer_sub).start()
             return carry
 
         lax.fori_loop(0, blocks, one, 0)
@@ -495,11 +510,51 @@
     def _():
         send_edges(1, sub - 1)
 
-    spread(y_a, got_a, s2, r2)
+    @pl.when(lax.rem(sub, 2) == 1)
+    def _():
+        send_third()
 
     for tile in range(tiles):
         if tile not in early:
             second(tile)
+
+    packed_row = iota((160, LANES), 0)
+    face_row = jnp.where(
+        packed_row < 104, packed_row,
+        jnp.where(iota((160, LANES), 1) < LANES // 2, packed_row - 104, packed_row - 48),
+    )
+
+    def sources(of):
+        wanted = jnp.full((160, LANES), -1.0, F32)
+        for q in range(4):
+            inside = (face_row >= q * FACE) & (face_row < (q + 1) * FACE)
+            wanted = jnp.where(inside, of[q ^ 1], wanted)
+        return wanted
+
+    first_block = (group * QUAD).astype(F32)
+
+    def from_group(wanted):
+        taken = jnp.zeros((160, LANES), F32)
+        for q in range(QUAD):
+            taken = jnp.where(wanted == first_block + float(q), faces[q], taken)
+        return taken
+
+    for step in range(1, QUAD):
+        whence = lax.rem(spot + step, QUAD)
+        face_copy(whence, whence).wait_recv()
+    for step in range(1, groups):
+        to = lax.rem(group + step, groups)
+        wanted = []
+        for k in range(4):
+            total = jnp.zeros((1, 1), F32)
+            for t in range(packs):
+                here = lane[0:1] + t * LANES == (to * QUAD + spot) * nrb + k
+                total = total + jnp.sum(
+                    jnp.where(here, first_pack[t][9:10], 0.0), 1, keepdims=True
+                )
+            wanted.append(total)
+        pass_msg[to] = from_group(sources(wanted))
+        pass_copy(group, to).start()
 
     unit = jnp.where(iota((PAD, trace), 0) == iota((PAD, trace), 1), 1.0, 0.0)
     r_high = restriction_high = spread_r[:, :trace].astype(BF16).astype(F32)
@@ -518,7 +573,7 @@
     both = lhs[...]
     weights = nt(
         both[:, :trace],
-        jnp.concatenate([base[:, :trace], jnp.zeros((8 * COARSE, trace), F32)], 0), HIGHEST,
+        jnp.concatenate([base[:, 0:trace], jnp.zeros((8 * COARSE, trace), F32)], 0), HIGHEST,
     )
     signs = jnp.where(iota((PAD, LANES), 1) < 4 * COARSE, -0.5, 0.5)
     rows_in = iota((PAD, LANES), 0) < trace
@@ -594,44 +649,6 @@
             total = total + pltpu.roll(values, LANES - k, 1)
         return jnp.where(in_block == 0, total, 0.0)
 
-    packed_row = iota((160, LANES), 0)
-    face_row = jnp.where(
-        packed_row < 104, packed_row,
-        jnp.where(iota((160, LANES), 1) < LANES // 2, packed_row - 104, packed_row - 48),
-    )
-
-    def sources(of):
-        wanted = jnp.full((160, LANES), -1.0, F32)
-        for q in range(4):
-            inside = (face_row >= q * FACE) & (face_row < (q + 1) * FACE)
-            wanted = jnp.where(inside, of[q ^ 1], wanted)
-        return wanted
-
-    first_block = (group * QUAD).astype(F32)
-
-    def from_group(wanted):
-        taken = jnp.zeros((160, LANES), F32)
-        for q in range(QUAD):
-            taken = jnp.where(wanted == first_block + float(q), faces[q], taken)
-        return taken
-
-    for step in range(1, QUAD):
-        whence = lax.rem(spot + step, QUAD)
-        face_copy(whence, whence).wait_recv()
-    for step in range(1, groups):
-        to = lax.rem(group + step, groups)
-        wanted = []
-        for k in range(4):
-            total = jnp.zeros((1, 1), F32)
-            for t in range(packs):
-                here = lane[0:1] + t * LANES == (to * QUAD + spot) * nrb + k
-                total = total + jnp.sum(
-                    jnp.where(here, first_pack[t][9:10], 0.0), 1, keepdims=True
-                )
-            wanted.append(total)
-        pass_msg[to] = from_group(sources(wanted))
-        pass_copy(group, to).start()
-
     collect(msg3, got3, s3, r3)
     third_pack = packed(got3)
     swapped = (in_block + 1 - 2 * lax.rem(in_block, 2)).astype(F32)[0:1]
@@ -645,11 +662,7 @@
     fetched = [0.5 * fetch(rows, slots_both[t], owners_both[t]) for t in range(packs)]
 
     def take_edges(slot, peer_sub):
-        def one(j, carry):
-            edge_copy(slot, lax.rem(me + j, blocks), lax.rem(me + j, blocks), peer_sub).wait_recv()
-            return carry
-
-        lax.fori_loop(0, blocks, one, 0)
+        all_edges(slot, peer_sub).wait_recv()
 
     @pl.when(sub > 0)
     def _():
@@ -774,11 +787,7 @@
     sent(msg3, got3, s3, r3)
 
     def edges_sent(slot, peer_sub):
-        def one(j, carry):
-            edge_copy(slot, me, lax.rem(me + j, blocks), peer_sub).wait_send()
-            return carry
-
-        lax.fori_loop(0, blocks, one, 0)
+        all_edges(slot, peer_sub).wait_send()
 
     @pl.when(sub < subs - 1)
     def _():
@@ -859,6 +868,7 @@
             pltpu.VMEM((PAD, elements + 2 * LANES), F32),
             pltpu.VMEM((PAD, width), F32),
             pltpu.VMEM((PAD, LANES), F32),
+            pltpu.VMEM((8 * COARSE, 2 * LANES), F32),
             pltpu.VMEM((16, LANES), F32),
             pltpu.VMEM((16, LANES), F32),
             pltpu.VMEM((blocks, 16, LANES), F32),
@@ -875,8 +885,8 @@
             pltpu.VMEM((blocks // QUAD, 160, LANES), F32),
             pltpu.VMEM((2, 56, LANES), F32),
         ]
-        + [dma((blocks,))] * 8
-        + [dma((2, blocks))] * 2
+        + [dma] * 8
+        + [dma((2,))] * 2
         + [dma((QUAD,))] * 2
         + [dma((2,))] * 2
         + [dma((blocks // QUAD,))] * 2

time: 22.9 us -> 21.9 us (0.956)
  Pallas kernels: 22.7 us -> 21.7 us
    pallas_call x1, Pallas kernels: 21.3 us -> 20.3 us  [per_device(): pl.pallas_call(functools.partial(kernel, blocks, subs), out_shape=(pltpu....]
where the time goes in v3:
time: 21.9 us; the launch traced here: 21.7 us
  Pallas kernels  21.7 us (99%)
    pallas_call x1, Pallas kernels, per_device(): pl.pallas_call(functools.partial(kernel, blocks, subs), out_shape=(pltpu....  20.3 us
    pallas_call x1, Pallas kernels, per_device(): pl.pallas_call(finish, out_shape=jax.ShapeDtypeStruct((trace, elements),...  1.4 us

profile of v3, /device:TPU:0, one launch (start us, length us, event | category | flops | bytes accessed | tf_op | source)
XLA Modules:
  0.0 21.7 jit_solution(5135906459174151244)
XLA Ops:
  0.0 20.3 %shard_map.91 = (f32[150,3072]{1,0:T(8,128)S(1)}, f32[152,128]{1,0:T(8,128)S(1)}) custom-call(s32[1,4]{1,0:T(1,128)} %partner_hbm.1, s32[1,4]{1,0:T(1,128)} %bitcast.6, s32[1,16]{1,0:T(1,128)} %bitcast.7, f32[150,3072]{1,0:T(8,128)} %rhs_hbm.1, f32[1,3072]{1,0:T(1,128)} %bitcast.5, f32[150,150]{1,0:T(8,128)} %s_ref_hbm.1, f32[150,150]{1,0:T(8,128)} %m_inv_hbm.1, ...), custom_call_target="tpu_custom_call" | custom-call | tf_op jit(solution)/shard_map/pallas_call | solution.py:844
  20.3 1.4 %shard_map.92 = f32[150,3072]{1,0:T(8,128)} custom-call(f32[152,128]{1,0:T(8,128)S(1)} %get-tuple-element.7.lift, f32[150,3072]{1,0:T(8,128)S(1)} %get-tuple-element.8.held), custom_call_target="tpu_custom_call" | custom-call | tf_op jit(solution)/shard_map/pallas_call | solution.py:901
